TPU v7x, 512 devices: a whole 4x8x8 slice. The times are simulated.
512 devices in a mesh: frame: 64 (over x, z_hi, y), row: 8 (over z_lo, core).
Axes of the slice: x: 4, y: 8, z: 8 (z_hi: 2, z_lo: 4; z = z_hi * 4 + z_lo), core: 2. Of those that a mesh axis runs over, the one named last changes fastest.
Arguments:
- latents: bfloat16 [256, 32, 32, 320], P('frame', 'row'), may hold values from -20 to 20
- ln_gain: bfloat16 [320], replicated, may hold values from 0.099609375 to 1.8984375
- q_weight: bfloat16 [320, 320], replicated, may hold values from -0.30078125 to 0.30078125
- k_weight: bfloat16 [320, 320], replicated, may hold values from -3 to 3
- v_weight: bfloat16 [320, 320], replicated, may hold values from -0.3125 to 0.3125
- o_weight: bfloat16 [320, 320], replicated, may hold values from -0.3125 to 0.3125
- gn_gain: bfloat16 [320], replicated, may hold values from 0.099609375 to 1.8984375
- conv_weight: bfloat16 [3, 3, 320, 320], replicated, may hold values from -0.109375 to 0.109375
- conv_bias: bfloat16 [320], replicated, may hold values from -3 to 3
Outputs:
- output: bfloat16 [256, 32, 32, 320], P('frame', 'row')
All inputs are finite; a program needn't handle non-finite values.
Results may differ from a plain program's by a relative error of at most 0.0085.
The roundings to bfloat16 on the way count: a program that leaves them out, or rounds other values in their place, can miss the bound.
Values may be sent and summed in bfloat16 or wider, within the bound.
A program may use at most 64 MiB of HBM per device.

v0:
```python
import math

import jax
import jax.numpy as jnp
from jax import lax
from jax.sharding import PartitionSpec as P

HEADS = 8
GROUPS = 32


def spread_2(value, axis, source):
    kept = jnp.where(lax.axis_index(axis) == source, value, 0).astype(value.dtype)
    return lax.psum(kept, axis)


def shifted(block, axis, distance):
    devices = range(lax.axis_size(axis))
    route = [(i - distance, i) for i in devices if i - distance in devices]
    return lax.ppermute(block, axis, route)


def with_halo(value, sides, width):
    for axis, dim in sides:
        size, length = (lax.axis_size(axis), value.shape[dim])
        up = [(i, (i + 1) % size) for i in range(size - 1)]
        down = [(j, i) for i, j in up]
        last = lax.slice_in_dim(value, length - width, length, axis=dim)
        leading = lax.slice_in_dim(value, 0, width, axis=dim)
        before = lax.ppermute(last, axis, up)
        after = lax.ppermute(leading, axis, down)
        value = jnp.concatenate([before, value, after], axis=dim)
    return value


def layer_normed(values, gain_vec):
    floated = values.astype(jnp.float32)
    centre = floated - jnp.mean(floated, axis=-1, keepdims=True)
    spread = jnp.mean(centre * centre, axis=-1, keepdims=True)
    return (centre * lax.rsqrt(spread + 1e-05) * gain_vec.astype(jnp.float32)).astype(jnp.bfloat16)


def attend_frames(queries, key_set, value_set, factor):
    lead_keys = key_set[0]
    lead_values = value_set[0]

    def single(operands):
        frame_queries, frame_keys, frame_values = operands
        all_keys = jnp.concatenate([lead_keys, frame_keys], axis=0)
        all_values = jnp.concatenate([lead_values, frame_values], axis=0)
        scores = (
            jnp.einsum("qhd,khd->hqk", frame_queries, all_keys, preferred_element_type=jnp.float32)
            * factor
        )
        highest = jnp.max(scores, axis=-1, keepdims=True)
        raised = jnp.exp(scores - highest)
        totals = jnp.sum(raised, axis=-1)
        summed = jnp.einsum(
            "hqk,khd->qhd",
            raised.astype(jnp.bfloat16),
            all_values,
            preferred_element_type=jnp.float32,
        )
        return (summed / jnp.transpose(totals)[:, :, None]).astype(jnp.bfloat16)

    return lax.map(single, (queries, key_set[1:], value_set[1:]))


def body(latents, ln_gain, q_weight, k_weight, v_weight, o_weight, gn_gain, conv_weight, conv_bias):
    frames, row_count, col_count, channels = latents.shape
    tok_shard = row_count * col_count
    head_dim = channels // HEADS
    factor = 1.0 / math.sqrt(head_dim)
    tokens = latents.reshape(frames * tok_shard, channels)
    kv_weight = jnp.concatenate([k_weight, v_weight], axis=1)
    normed = layer_normed(tokens, ln_gain)
    queries = jnp.dot(normed, q_weight, preferred_element_type=jnp.float32).astype(jnp.bfloat16)
    queries = queries.reshape(frames, tok_shard, channels)
    paired = jnp.dot(normed, kv_weight, preferred_element_type=jnp.float32).astype(jnp.bfloat16)
    paired = paired.reshape(frames, tok_shard, 2 * channels)
    leading = spread_2(paired[0], "frame", 0)
    earlier = shifted(paired[frames - 1], "frame", 1)
    earlier = jnp.where(lax.axis_index("frame") == 0, paired[0], earlier)
    stacked = jnp.concatenate([leading[None], earlier[None], paired[: frames - 1]], axis=0)
    sent_queries = queries.reshape(frames, tok_shard, 1, HEADS, head_dim)
    sent_pairs = stacked.reshape(frames + 1, tok_shard, 2, HEADS, head_dim)
    got_queries, got_pairs = (
        lax.all_to_all(sent_queries, "row", split_axis=3, concat_axis=1, tiled=True),
        lax.all_to_all(sent_pairs, "row", split_axis=3, concat_axis=1, tiled=True),
    )
    head_results = attend_frames(
        got_queries[:, :, 0], got_pairs[:, :, 0], got_pairs[:, :, 1], factor
    )
    returned = lax.all_to_all(head_results, "row", split_axis=1, concat_axis=2, tiled=True)
    attended = returned.reshape(frames * tok_shard, channels)
    mixed = jnp.dot(attended, o_weight, preferred_element_type=jnp.float32)
    updated = (tokens.astype(jnp.float32) + mixed).astype(jnp.bfloat16)
    group_width = channels // GROUPS
    grouped = updated.astype(jnp.float32).reshape(frames, tok_shard, GROUPS, group_width)
    sum_parts = jnp.sum(grouped, axis=(1, 3))
    square_parts = jnp.sum(grouped * grouped, axis=(1, 3))
    group_sum, group_square = lax.psum((sum_parts, square_parts), "row")
    counted = tok_shard * lax.axis_size("row") * group_width
    group_mean = group_sum / counted
    group_var = group_square / counted - group_mean * group_mean
    scaled = (grouped - group_mean[:, None, :, None]) * lax.rsqrt(group_var + 1e-05)[
        :, None, :, None
    ]
    activated = jax.nn.silu(
        scaled.reshape(frames, tok_shard, channels) * gn_gain.astype(jnp.float32)
    )
    activated = activated.astype(jnp.bfloat16).reshape(frames, row_count, col_count, channels)
    padded = with_halo(activated, (("row", 1),), 1)
    padded = jnp.pad(padded, ((0, 0), (0, 0), (1, 1), (0, 0)))
    convolved = jnp.zeros((frames * tok_shard, channels), jnp.float32)
    for row_off in range(3):
        for col_off in range(3):
            window = padded[
                :, row_off : row_off + row_count, col_off : col_off + col_count, :
            ].reshape(frames * tok_shard, channels)
            convolved = convolved + jnp.dot(
                window, conv_weight[row_off, col_off], preferred_element_type=jnp.float32
            )
    output = updated.astype(jnp.float32) + convolved + conv_bias.astype(jnp.float32)
    return output.astype(jnp.bfloat16).reshape(frames, row_count, col_count, channels)


def solution(mesh):
    in_specs = (P("frame", "row", None, None), P(), P(), P(), P(), P(), P(), P(), P())
    out_specs = P("frame", "row", None, None)
    return jax.shard_map(body, mesh=mesh, in_specs=in_specs, out_specs=out_specs, check_vma=False)
```

profile of v0, /device:TPU:1, one launch (start us, length us, event | category | flops | bytes accessed | tf_op | source)
XLA Modules:
  0.0 901.8 jit_solution(13939154227271930684)
XLA Ops:
  6.5 1.2 convert_reduce_fusion
  7.8 1.3 multiply_reduce_fusion.1
  9.2 0.7 convert_element_type.63
  9.9 1.2 multiply_convert_fusion.1
  11.1 0.4 convolution_convert_fusion.1
  11.6 0.8 copy.107
  12.4 10.2 %all-to-all-start.1 = ((bf16[4,128,1,8,40]{1,4,0,2,3:T(8,128)(2,1)}), bf16[4,128,1,8,40]{1,4,0,2,3:T(8,128)(2,1)S(1)}, u32[]{:S(2)}, u32[]{:S(2)}) async-start(bf16[4,128,1,8,40]{1,4,0,2,3:T(8,128)(2,1)} %copy.107), calls=%async_computation.1 | async-start | bytes 655360 | tf_op jit(solution)/shard_map/all_to_all | solution.py:88
  22.6 0.6 convolution_convert_fusion
  23.2 1.8 collective-permute-start
  25.0 0.8 copy.100
  25.9 0.3 copy.102
  26.3 2.2 collective-permute-done
  28.7 0.3 copy.104
  29.0 741.8 %all-reduce.4.cloned.1.call-done = bf16[1,128,2,8,40]{1,4,3,2,0:T(8,128)(2,1)} async-done(((bf16[1,128,2,8,40]{1,4,3,2,0:T(8,128)(2,1)}), bf16[1,128,2,8,40]{1,4,3,2,0:T(8,128)(2,1)}) %all-reduce.4.cloned.1.call-update) | async-done | bytes 163856 | tf_op jit(solution)/shard_map/psum | solution.py:14
  770.9 1.2 copy.103
  772.0 1.1 pad_maximum_fusion
  773.1 1.0 copy.105
  774.1 27.1 %all-to-all-start = ((bf16[5,128,2,8,40]{1,4,2,0,3:T(8,128)(2,1)}), bf16[5,128,2,8,40]{1,4,2,0,3:T(8,128)(2,1)S(1)}, u32[]{:S(2)}, u32[]{:S(2)}) async-start(bf16[5,128,2,8,40]{1,4,2,0,3:T(8,128)(2,1)} %copy.105), calls=%async_computation | async-start | bytes 1638400 | tf_op jit(solution)/shard_map/all_to_all | solution.py:89
  801.5 20.5 %all-to-all-done = bf16[5,128,2,8,40]{1,4,2,0,3:T(8,128)(2,1)S(1)} async-done(((bf16[5,128,2,8,40]{1,4,2,0,3:T(8,128)(2,1)}), bf16[5,128,2,8,40]{1,4,2,0,3:T(8,128)(2,1)S(1)}, u32[]{:S(2)}, u32[]{:S(2)}) %all-to-all-start) | async-done | bytes 819232 | tf_op jit(solution)/shard_map/all_to_all | solution.py:89
  822.2 19.6 %while.10 = (s32[]{:T(128)}, bf16[4,1024,1,40]{1,3,2,0:T(8,128)(2,1)S(1)}, bf16[4,1024,1,40]{1,3,2,0:T(8,128)(2,1)S(1)}, bf16[1024,1,40]{0,2,1:T(8,128)(2,1)S(1)...) while((s32[]{:T(128)}, ...), condition=%wide.region_6.7_spmd, body=%wide.region_3.6_spmd.sunk | while | flops 353056768 | bytes 26005600 | solution.py:66
  822.3 1.4 multiply_reduce_fusion.4
  823.6 1.9 fusion.91
  825.6 1.5 fusion.92
  827.2 1.4 multiply_reduce_fusion.4
  828.5 1.9 fusion.91
  830.5 1.5 fusion.92
  832.1 1.4 multiply_reduce_fusion.4
  833.4 1.9 fusion.91
  835.4 1.5 fusion.92
  837.0 1.4 multiply_reduce_fusion.4
  838.3 1.9 fusion.91
  840.3 1.5 fusion.92
  841.8 0.7 copy.110
  842.6 2.3 reshape.146
  844.9 4.2 all-to-all-start.2
  849.3 9.8 %all-to-all-done.2 = bf16[8,2,10240]{2,1,0:T(2,128)(2,1)S(1)} async-done(((bf16[8,2,10240]{2,1,0:T(2,128)(2,1)}), bf16[8,2,10240]{2,1,0:T(2,128)(2,1)S(1)}, u32[]{:S(2)}, u32[]{:S(2)}) %all-to-all-start.2) | async-done | bytes 327712 | tf_op jit(solution)/shard_map/all_to_all | solution.py:94
  859.1 1.6 reshape.147
  860.7 0.6 copy.120
  861.3 0.3 copy.112
  861.6 0.4 fusion.36
  862.3 0.3 copy.114
  862.5 0.3 fusion.71
  863.0 14.1 %all-reduce.1 = (f32[4,32]{1,0:T(4,128)S(1)}, f32[4,32]{1,0:T(4,128)S(1)}) all-reduce(f32[4,32]{1,0:T(4,128)S(1)} %copy.116, f32[4,32]{1,0:T(4,128)S(1)} %copy.115), channel_id=1, replica_groups=mesh['frame'=64,'row'=8] {'row'}, use_global_device_ids=true, to_apply=%region_10.11 | all-reduce | flops 256 | bytes 2048 | tf_op jit(solution)/shard_map/psum | solution.py:102
  877.4 0.2 multiply_convert_fusion
  877.7 0.7 fusion.73
  878.4 1.9 collective-permute-start.1
  880.3 2.8 collective-permute-start.2
  883.2 0.2 copy.117
  883.5 0.2 copy.118
  883.8 2.7 collective-permute-done.2
  886.6 1.2 fusion.41
  887.8 0.4 fusion.72
  888.2 1.2 copy-done.2
  889.4 0.4 fusion.58
  889.8 0.4 fusion.49
  890.2 1.0 pad_maximum_fusion.1
  891.2 0.4 convolution_add_fusion.6
  891.6 0.4 convolution_add_fusion.5
  891.9 0.4 convolution_add_fusion.4
  892.3 0.5 convolution_add_fusion.3
  892.9 0.4 convolution_add_fusion.2
  893.3 0.4 convolution_add_fusion.1
  893.7 0.4 fusion.35
  894.1 0.9 copy.119
  (52 shorter events, 2.3 us)
Async XLA Ops:
  6.5 4.6 copy-start
  6.5 16.1 %copy-start.7 = (bf16[320,320]{1,0:T(8,128)(2,1)S(1)}, bf16[320,320]{1,0:T(8,128)(2,1)}, u32[]{:S(2)}) copy-start(bf16[320,320]{1,0:T(8,128)(2,1)} %param.14) | copy-start | bytes 614404
  6.5 16.1 %copy-start.6 = (bf16[320,320]{1,0:T(8,128)(2,1)S(1)}, bf16[320,320]{1,0:T(8,128)(2,1)}, u32[]{:S(2)}) copy-start(bf16[320,320]{1,0:T(8,128)(2,1)} %param.15) | copy-start | bytes 614404
  12.4 761.8 %all-to-all-start.1 = ((bf16[4,128,1,8,40]{1,4,0,2,3:T(8,128)(2,1)}), bf16[4,128,1,8,40]{1,4,0,2,3:T(8,128)(2,1)S(1)}, u32[]{:S(2)}, u32[]{:S(2)}) async-start(bf16[4,128,1,8,40]{1,4,0,2,3:T(8,128)(2,1)} %copy.107), calls=%async_computation.1 | async-start | bytes 655360 | tf_op jit(solution)/shard_map/all_to_all | solution.py:88
  22.6 748.3 %all-reduce.4.cloned.1.call-start = ((), (), s32[]{:S(2)}) async-start(), calls=%async_computation.3 | async-start | bytes 327680 | tf_op jit(solution)/shard_map/psum | solution.py:14
  23.2 5.3 collective-permute-start
  774.1 47.9 %all-to-all-start = ((bf16[5,128,2,8,40]{1,4,2,0,3:T(8,128)(2,1)}), bf16[5,128,2,8,40]{1,4,2,0,3:T(8,128)(2,1)S(1)}, u32[]{:S(2)}, u32[]{:S(2)}) async-start(bf16[5,128,2,8,40]{1,4,2,0,3:T(8,128)(2,1)} %copy.105), calls=%async_computation | async-start | bytes 1638400 | tf_op jit(solution)/shard_map/all_to_all | solution.py:89
  841.8 7.2 copy-start.1
  841.8 7.4 copy-start.4
  844.9 14.2 %all-to-all-start.2 = ((bf16[8,2,10240]{2,1,0:T(2,128)(2,1)}), bf16[8,2,10240]{2,1,0:T(2,128)(2,1)S(1)}, u32[]{:S(2)}, u32[]{:S(2)}) async-start(bf16[8,2,10240]{2,1,0:T(2,128)(2,1)} %reshape.146), calls=%async_computation.2 | async-start | bytes 655360 | tf_op jit(solution)/shard_map/all_to_all | solution.py:94
  849.1 12.6 %copy-start.3 = (bf16[320,320]{1,0:T(8,128)(2,1)S(1)}, bf16[320,320]{1,0:T(8,128)(2,1)}, u32[]{:S(2)}) copy-start(bf16[320,320]{1,0:T(8,128)(2,1)} %param.16) | copy-start | bytes 614404
  862.2 20.9 %copy-start.5 = (bf16[320]{0:T(512)(128)(2,1)S(1)}, bf16[320]{0:T(512)(128)(2,1)}, u32[]{:S(2)}) copy-start(bf16[320]{0:T(512)(128)(2,1)} %param.19) | copy-start | bytes 1924
  878.4 5.4 collective-permute-start.1
  880.3 6.3 collective-permute-start.2
  887.8 1.6 copy-start.2
Sparse Core Ops, SparseCore 0:
  26.3 744.4 all-reduce.3
where the time goes:
time: 902 us
  waiting for transfers between devices  777 us (86%)
  starting transfers between devices  48 us (5%)
  matrix products  16.6 us (2%)
  other arithmetic  16.1 us (2%)
  local copies, waits for them, and re-layouts  15.9 us (2%)
  blocking collectives  14.1 us (2%)
  between operations  13.9 us (2%)
    psum x1, waiting for transfers between devices, spread_2(): return lax.psum(kept, axis)  742 us
    all_to_all x1, starting transfers between devices, body(): lax.all_to_all(sent_pairs, 'row', split_axis=3, concat_axis=1, tiled=True)  27.1 us
    all_to_all x1, waiting for transfers between devices, body(): lax.all_to_all(sent_pairs, 'row', split_axis=3, concat_axis=1, tiled=True)  20.5 us
  transfers between devices with their start and end apart: 7, of which 5 were waited for; matrix products, arithmetic and copies ran while one was open for 1% of the time, Pallas kernels for 0%

commit v1 on v0

--- a/solution.py
+++ b/solution.py
@@ -10,8 +10,15 @@
 
 
 def spread_2(value, axis, source):
-    kept = jnp.where(lax.axis_index(axis) == source, value, 0).astype(value.dtype)
-    return lax.psum(kept, axis)
+    size = lax.axis_size(axis)
+    place = lax.axis_index(axis)
+    reach = 1
+    while reach < size:
+        route = [(i, i + reach) for i in range(min(reach, size - reach))]
+        got = lax.ppermute(value, axis, route)
+        value = jnp.where((place >= reach) & (place < 2 * reach), got, value)
+        reach *= 2
+    return value
 
 
 def shifted(block, axis, distance):

time: 902 us -> 163 us (0.18)
  the two profiles are of different devices: /device:TPU:1 before, /device:TPU:41 now
where the time goes in v1:
time: 163 us; the launch traced here: 162 us
  waiting for transfers between devices  64 us (39%)
  starting transfers between devices  34.9 us (21%)
  matrix products  17.6 us (11%)
  other arithmetic  16.1 us (10%)
  local copies, waits for them, and re-layouts  14.4 us (9%)
  blocking collectives  14.1 us (9%)
    ppermute x6, waiting for transfers between devices, spread_2(): got = lax.ppermute(value, axis, route)  24 us
    all_to_all x1, waiting for transfers between devices, body(): lax.all_to_all(sent_pairs, 'row', split_axis=3, concat_axis=1, tiled=True)  20.6 us
    psum x1, blocking collectives, body(): group_sum, group_square = lax.psum((sum_parts, square_parts), 'row')  14.1 us
    all_to_all x1, starting transfers between devices, body(): lax.all_to_all(sent_queries, 'row', split_axis=3, concat_axis=1, tiled=True)  12.5 us
    all_to_all x1, waiting for transfers between devices, body(): lax.all_to_all(head_results, 'row', split_axis=1, concat_axis=2, tiled=True)  9.84 us
    reduce_sum x4, other arithmetic, single(): totals = jnp.sum(raised, axis=-1)  7.73 us
    ppermute x6, starting transfers between devices, spread_2(): got = lax.ppermute(value, axis, route)  6.53 us
    dot_general x4, matrix products, single(): jnp.einsum('hqk,khd->qhd', raised.astype(jnp.bfloat16), all_values, prefe...  6.14 us
  transfers between devices with their start and end apart: 12, of which 8 were waited for; matrix products, arithmetic and copies ran while one was open for 4% of the time, Pallas kernels for 0%

profile of v1, /device:TPU:41, one launch (start us, length us, event | category | flops | bytes accessed | tf_op | source)
XLA Modules:
  0.0 161.9 jit_solution(1683584132101429680)
XLA Ops:
  0.0 1.2 convert_reduce_fusion
  1.2 1.3 multiply_reduce_fusion.1
  2.7 0.7 convert_element_type.61
  3.4 1.2 multiply_convert_fusion.1
  4.6 1.6 %convolution_convert_fusion = bf16[512,640]{1,0:T(8,128)(2,1)S(1)} fusion(bf16[512,320]{1,0:T(8,128)(2,1)S(1)} %multiply_convert_fusion.1, bf16[320,320]{1,0:T(8,128)(2,1)} %param.15, bf16[320,320]{1,0:T(8,128)(2,1)} %param.14), kind=kOutput, calls=%fused_computation.28 | convolution fusion | flops 210862080 | bytes 1392640 | tf_op jit(solution)/shard_map/dot_general | solution.py:86
  6.3 0.7 collective-permute-start
  6.9 2.3 %collective-permute-start.6 = (bf16[128,640]{1,0:T(8,128)(2,1)S(1)}, bf16[128,640]{1,0:T(8,128)(2,1)S(1)}, u32[]{:S(2)}, u32[]{:S(2)}) collective-permute-start(bf16[128,640]{1,0:T(8,128)(2,1)S(1)} %get-tuple-element.120), channel_id=1, source_target_pairs={{0,8},{8,16},{16,24},{24,32},{32,40},{40,48},{48,56},{56,64},{64,7... | collective-permute-start | bytes 491528 | tf_op jit(solution)/shard_map/ppermute | solution.py:27
  9.3 4.6 %collective-permute-done.6 = bf16[128,640]{1,0:T(8,128)(2,1)S(1)} collective-permute-done((bf16[128,640]{1,0:T(8,128)(2,1)S(1)}, bf16[128,640]{1,0:T(8,128)(2,1)S(1)}, u32[]{:S(2)}, u32[]{:S(2)}) %collective-permute-start.6) | collective-permute-done | bytes 163872 | tf_op jit(solution)/shard_map/ppermute | solution.py:27
  13.9 0.7 collective-permute-start.1
  14.7 1.3 collective-permute-start.2
  16.0 18.9 %collective-permute-done.2 = bf16[128,640]{1,0:T(8,128)(2,1)S(1)} collective-permute-done((bf16[128,640]{1,0:T(8,128)(2,1)S(1)}, bf16[128,640]{1,0:T(8,128)(2,1)S(1)}, u32[]{:S(2)}, u32[]{:S(2)}) %collective-permute-start.2) | collective-permute-done | bytes 163872 | tf_op jit(solution)/shard_map/ppermute | solution.py:18
  34.9 1.3 collective-permute-start.3
  36.2 2.2 %collective-permute-done.3 = bf16[128,640]{1,0:T(8,128)(2,1)S(1)} collective-permute-done((bf16[128,640]{1,0:T(8,128)(2,1)S(1)}, bf16[128,640]{1,0:T(8,128)(2,1)S(1)}, u32[]{:S(2)}, u32[]{:S(2)}) %collective-permute-start.3) | collective-permute-done | bytes 163872 | tf_op jit(solution)/shard_map/ppermute | solution.py:18
  38.4 1.3 collective-permute-start.4
  39.8 0.4 convolution_convert_fusion.1
  40.2 0.8 copy.107
  41.0 12.5 %all-to-all-start.1 = ((bf16[4,128,1,8,40]{1,4,0,2,3:T(8,128)(2,1)}), bf16[4,128,1,8,40]{1,4,0,2,3:T(8,128)(2,1)S(1)}, u32[]{:S(2)}, u32[]{:S(2)}) async-start(bf16[4,128,1,8,40]{1,4,0,2,3:T(8,128)(2,1)} %copy.107), calls=%async_computation.1 | async-start | bytes 655360 | tf_op jit(solution)/shard_map/all_to_all | solution.py:95
  53.6 1.3 collective-permute-start.5
  55.8 2.9 %collective-permute-done.5 = bf16[128,640]{1,0:T(8,128)(2,1)S(1)} collective-permute-done((bf16[128,640]{1,0:T(8,128)(2,1)S(1)}, bf16[128,640]{1,0:T(8,128)(2,1)S(1)}, u32[]{:S(2)}, u32[]{:S(2)}) %collective-permute-start.5) | collective-permute-done | bytes 163872 | tf_op jit(solution)/shard_map/ppermute | solution.py:18
  59.1 1.1 pad_maximum_fusion
  60.2 1.0 copy.105
  61.3 2.3 %all-to-all-done.1 = bf16[4,128,1,8,40]{1,4,0,2,3:T(8,128)(2,1)S(1)} async-done(((bf16[4,128,1,8,40]{1,4,0,2,3:T(8,128)(2,1)}), bf16[4,128,1,8,40]{1,4,0,2,3:T(8,128)(2,1)S(1)}, u32[]{:S(2)}, u32[]{:S(2)}) %all-to-all-start.1) | async-done | bytes 327712 | tf_op jit(solution)/shard_map/all_to_all | solution.py:95
  63.6 4.6 %all-to-all-start = ((bf16[5,128,2,8,40]{1,4,2,0,3:T(8,128)(2,1)}), bf16[5,128,2,8,40]{1,4,2,0,3:T(8,128)(2,1)S(1)}, u32[]{:S(2)}, u32[]{:S(2)}) async-start(bf16[5,128,2,8,40]{1,4,2,0,3:T(8,128)(2,1)} %copy.105), calls=%async_computation | async-start | bytes 1638400 | tf_op jit(solution)/shard_map/all_to_all | solution.py:96
  68.4 20.6 %all-to-all-done = bf16[5,128,2,8,40]{1,4,2,0,3:T(8,128)(2,1)S(1)} async-done(((bf16[5,128,2,8,40]{1,4,2,0,3:T(8,128)(2,1)}), bf16[5,128,2,8,40]{1,4,2,0,3:T(8,128)(2,1)S(1)}, u32[]{:S(2)}, u32[]{:S(2)}) %all-to-all-start) | async-done | bytes 819232 | tf_op jit(solution)/shard_map/all_to_all | solution.py:96
  89.2 19.6 %while.10 = (s32[]{:T(128)}, bf16[4,1024,1,40]{1,3,2,0:T(8,128)(2,1)S(1)}, bf16[4,1024,1,40]{1,3,2,0:T(8,128)(2,1)S(1)}, bf16[1024,1,40]{0,2,1:T(8,128)(2,1)S(1)...) while((s32[]{:T(128)}, ...), condition=%wide.region_5.6_spmd, body=%wide.region_2.5_spmd.sunk | while | flops 353056768 | bytes 26005600 | solution.py:73
  89.2 1.4 multiply_reduce_fusion.4
  90.6 1.9 %fusion.92 = f32[1024]{0:T(1024)S(1)} fusion(f32[1024,2048]{1,0:T(8,128)S(1)} %get-tuple-element.175, f32[1024]{0:T(1024)S(1)} %get-tuple-element.176), kind=kLoop, calls=%fused_computation.2.clone.1 | loop fusion | flops 6290432 | bytes 8396800 | tf_op jit(solution)/shard_map/while/body/eval_jaxpr/reduce_sum | solution.py:64
  92.5 1.5 fusion.93
  94.1 1.4 multiply_reduce_fusion.4
  95.5 1.9 %fusion.92 = f32[1024]{0:T(1024)S(1)} fusion(f32[1024,2048]{1,0:T(8,128)S(1)} %get-tuple-element.175, f32[1024]{0:T(1024)S(1)} %get-tuple-element.176), kind=kLoop, calls=%fused_computation.2.clone.1 | loop fusion | flops 6290432 | bytes 8396800 | tf_op jit(solution)/shard_map/while/body/eval_jaxpr/reduce_sum | solution.py:64
  97.4 1.5 fusion.93
  99.0 1.4 multiply_reduce_fusion.4
  100.4 1.9 %fusion.92 = f32[1024]{0:T(1024)S(1)} fusion(f32[1024,2048]{1,0:T(8,128)S(1)} %get-tuple-element.175, f32[1024]{0:T(1024)S(1)} %get-tuple-element.176), kind=kLoop, calls=%fused_computation.2.clone.1 | loop fusion | flops 6290432 | bytes 8396800 | tf_op jit(solution)/shard_map/while/body/eval_jaxpr/reduce_sum | solution.py:64
  102.3 1.5 fusion.93
  103.9 1.4 multiply_reduce_fusion.4
  105.2 1.9 %fusion.92 = f32[1024]{0:T(1024)S(1)} fusion(f32[1024,2048]{1,0:T(8,128)S(1)} %get-tuple-element.175, f32[1024]{0:T(1024)S(1)} %get-tuple-element.176), kind=kLoop, calls=%fused_computation.2.clone.1 | loop fusion | flops 6290432 | bytes 8396800 | tf_op jit(solution)/shard_map/while/body/eval_jaxpr/reduce_sum | solution.py:64
  107.2 1.5 fusion.93
  108.8 0.7 copy.110
  109.5 2.3 %reshape.146 = bf16[8,2,10240]{2,1,0:T(2,128)(2,1)} reshape(bf16[1024,1,4,40]{3,2,1,0:T(4,128)(2,1)S(1)} %bitcast.143) | data formatting | bytes 655360
  111.8 4.2 %all-to-all-start.2 = ((bf16[8,2,10240]{2,1,0:T(2,128)(2,1)}), bf16[8,2,10240]{2,1,0:T(2,128)(2,1)S(1)}, u32[]{:S(2)}, u32[]{:S(2)}) async-start(bf16[8,2,10240]{2,1,0:T(2,128)(2,1)} %reshape.146), calls=%async_computation.2 | async-start | bytes 655360 | tf_op jit(solution)/shard_map/all_to_all | solution.py:101
  116.2 9.8 %all-to-all-done.2 = bf16[8,2,10240]{2,1,0:T(2,128)(2,1)S(1)} async-done(((bf16[8,2,10240]{2,1,0:T(2,128)(2,1)}), bf16[8,2,10240]{2,1,0:T(2,128)(2,1)S(1)}, u32[]{:S(2)}, u32[]{:S(2)}) %all-to-all-start.2) | async-done | bytes 327712 | tf_op jit(solution)/shard_map/all_to_all | solution.py:101
  126.0 1.6 %reshape.147 = bf16[1024,1,4,40]{3,2,1,0:T(4,128)(2,1)S(1)} reshape(bf16[8,2,10240]{2,1,0:T(2,128)(2,1)S(1)} %all-to-all-done.2) | data formatting | bytes 655360
  127.7 0.6 copy.120
  128.5 0.4 fusion.36
  129.4 0.3 fusion.71
  129.9 14.1 %all-reduce.1 = (f32[4,32]{1,0:T(4,128)S(1)}, f32[4,32]{1,0:T(4,128)S(1)}) all-reduce(f32[4,32]{1,0:T(4,128)S(1)} %copy.116, f32[4,32]{1,0:T(4,128)S(1)} %copy.115), channel_id=1, replica_groups=mesh['frame'=64,'row'=8] {'row'}, use_global_device_ids=true, to_apply=%region_9.10 | all-reduce | flops 256 | bytes 2048 | tf_op jit(solution)/shard_map/psum | solution.py:109
  144.6 0.7 fusion.74
  145.3 1.9 %collective-permute-start.7 = (bf16[4,1,32,320]{3,2,1,0:T(8,128)(2,1)}, bf16[4,1,32,320]{3,2,1,0:T(8,128)(2,1)S(1)}, u32[]{:S(2)}, u32[]{:S(2)}) collective-permute-start(bf16[4,1,32,320]{3,2,1,0:T(8,128)(2,1)} %get-tuple-element.123), channel_id=1, source_target_pairs={{0,1},{1,2},{2,3},{3,4},{4,5},{5,6},{6,7},{8,9},{9,10},{10,11},{11... | collective-permute-start | bytes 245768 | tf_op jit(solution)/shard_map/ppermute | solution.py:37
  147.2 2.8 %collective-permute-start.8 = (bf16[4,1,32,320]{3,2,1,0:T(8,128)(2,1)}, bf16[4,1,32,320]{3,2,1,0:T(8,128)(2,1)}, u32[]{:S(2)}, u32[]{:S(2)}) collective-permute-start(bf16[4,1,32,320]{3,2,1,0:T(8,128)(2,1)} %get-tuple-element.124), channel_id=1, source_target_pairs={{1,0},{2,1},{3,2},{4,3},{5,4},{6,5},{7,6},{9,8},{10,9},{11,10},{12... | collective-permute-start | bytes 245768 | tf_op jit(solution)/shard_map/ppermute | solution.py:38
  150.7 2.7 %collective-permute-done.8 = bf16[4,1,32,320]{3,2,1,0:T(8,128)(2,1)} collective-permute-done((bf16[4,1,32,320]{3,2,1,0:T(8,128)(2,1)}, bf16[4,1,32,320]{3,2,1,0:T(8,128)(2,1)}, u32[]{:S(2)}, u32[]{:S(2)}) %collective-permute-start.8) | collective-permute-done | bytes 81952 | tf_op jit(solution)/shard_map/ppermute | solution.py:38
  153.5 1.2 fusion.41
  154.7 0.4 fusion.72
  155.1 1.2 copy-done.2
  156.3 0.4 fusion.58
  156.7 0.4 fusion.49
  157.1 1.0 pad_maximum_fusion.1
  158.1 0.4 convolution_add_fusion.6
  158.5 0.4 convolution_add_fusion.5
  158.9 0.4 convolution_add_fusion.4
  159.2 0.5 convolution_add_fusion.3
  159.8 0.4 convolution_add_fusion.2
  160.2 0.4 convolution_add_fusion.1
  160.6 0.4 fusion.35
  161.0 0.9 copy.119
  (62 shorter events, 4.6 us)
Async XLA Ops:
  0.0 39.7 %copy-start = (bf16[320,320]{1,0:T(8,128)(2,1)S(1)}, bf16[320,320]{1,0:T(8,128)(2,1)}, u32[]{:S(2)}) copy-start(bf16[320,320]{1,0:T(8,128)(2,1)} %param.13) | copy-start | bytes 614404
  6.3 3.0 %collective-permute-start = (bf16[128,640]{1,0:T(8,128)(2,1)S(1)}, bf16[128,640]{1,0:T(8,128)(2,1)S(1)}, u32[]{:S(2)}, u32[]{:S(2)}) collective-permute-start(bf16[128,640]{1,0:T(8,128)(2,1)S(1)} %get-tuple-element.119), channel_id=1, source_target_pairs={{0,8},{1,9},{2,10},{3,11},{4,12},{5,13},{6,14},{7,15}} | collective-permute-start | bytes 491528 | tf_op jit(solution)/shard_map/ppermute | solution.py:18
  6.9 7.0 %collective-permute-start.6 = (bf16[128,640]{1,0:T(8,128)(2,1)S(1)}, bf16[128,640]{1,0:T(8,128)(2,1)S(1)}, u32[]{:S(2)}, u32[]{:S(2)}) collective-permute-start(bf16[128,640]{1,0:T(8,128)(2,1)S(1)} %get-tuple-element.120), channel_id=1, source_target_pairs={{0,8},{8,16},{16,24},{24,32},{32,40},{40,48},{48,56},{56,64},{64,7... | collective-permute-start | bytes 491528 | tf_op jit(solution)/shard_map/ppermute | solution.py:27
  13.9 0.7 collective-permute-start.1
  14.7 20.2 %collective-permute-start.2 = (bf16[128,640]{1,0:T(8,128)(2,1)S(1)}, bf16[128,640]{1,0:T(8,128)(2,1)S(1)}, u32[]{:S(2)}, u32[]{:S(2)}) collective-permute-start(bf16[128,640]{1,0:T(8,128)(2,1)S(1)} %broadcast_select_fusion.2), channel_id=1, source_target_pairs={{0,32},{8,40},{16,48},{24,56},{1,33},{9,41},{17,49},{25,57},{2,34}... | collective-permute-start | bytes 491528 | tf_op jit(solution)/shard_map/ppermute | solution.py:18
  34.9 3.5 %collective-permute-start.3 = (bf16[128,640]{1,0:T(8,128)(2,1)S(1)}, bf16[128,640]{1,0:T(8,128)(2,1)S(1)}, u32[]{:S(2)}, u32[]{:S(2)}) collective-permute-start(bf16[128,640]{1,0:T(8,128)(2,1)S(1)} %broadcast_select_fusion.3), channel_id=1, source_target_pairs={{0,64},{8,72},{16,80},{24,88},{32,96},{40,104},{48,112},{56,120},{... | collective-permute-start | bytes 491528 | tf_op jit(solution)/shard_map/ppermute | solution.py:18
  38.4 15.1 %collective-permute-start.4 = (bf16[128,640]{1,0:T(8,128)(2,1)S(1)}, bf16[128,640]{1,0:T(8,128)(2,1)S(1)}, u32[]{:S(2)}, u32[]{:S(2)}) collective-permute-start(bf16[128,640]{1,0:T(8,128)(2,1)S(1)} %broadcast_select_fusion.4), channel_id=1, source_target_pairs={{0,128},{8,136},{16,144},{24,152},{32,160},{40,168},{48,176},{56,1... | collective-permute-start | bytes 491528 | tf_op jit(solution)/shard_map/ppermute | solution.py:18
  41.0 22.6 %all-to-all-start.1 = ((bf16[4,128,1,8,40]{1,4,0,2,3:T(8,128)(2,1)}), bf16[4,128,1,8,40]{1,4,0,2,3:T(8,128)(2,1)S(1)}, u32[]{:S(2)}, u32[]{:S(2)}) async-start(bf16[4,128,1,8,40]{1,4,0,2,3:T(8,128)(2,1)} %copy.107), calls=%async_computation.1 | async-start | bytes 655360 | tf_op jit(solution)/shard_map/all_to_all | solution.py:95
  53.6 5.1 %collective-permute-start.5 = (bf16[128,640]{1,0:T(8,128)(2,1)S(1)}, bf16[128,640]{1,0:T(8,128)(2,1)S(1)}, u32[]{:S(2)}, u32[]{:S(2)}) collective-permute-start(bf16[128,640]{1,0:T(8,128)(2,1)S(1)} %broadcast_select_fusion.5), channel_id=1, source_target_pairs={{0,256},{8,264},{16,272},{24,280},{32,288},{40,296},{48,304},{56,3... | collective-permute-start | bytes 491528 | tf_op jit(solution)/shard_map/ppermute | solution.py:18
  63.6 25.4 %all-to-all-start = ((bf16[5,128,2,8,40]{1,4,2,0,3:T(8,128)(2,1)}), bf16[5,128,2,8,40]{1,4,2,0,3:T(8,128)(2,1)S(1)}, u32[]{:S(2)}, u32[]{:S(2)}) async-start(bf16[5,128,2,8,40]{1,4,2,0,3:T(8,128)(2,1)} %copy.105), calls=%async_computation | async-start | bytes 1638400 | tf_op jit(solution)/shard_map/all_to_all | solution.py:96
  108.7 7.2 %copy-start.1 = (bf16[4,4,32,320]{3,2,1,0:T(8,128)(2,1)S(1)}, bf16[4,4,32,320]{3,2,1,0:T(8,128)(2,1)}, u32[]{:S(2)}) copy-start(bf16[4,4,32,320]{3,2,1,0:T(8,128)(2,1)} %param.11) | copy-start | bytes 983044
  108.7 7.4 %copy-start.4 = (bf16[320]{0:T(512)(128)(2,1)S(1)}, bf16[320]{0:T(512)(128)(2,1)}, u32[]{:S(2)}) copy-start(bf16[320]{0:T(512)(128)(2,1)} %param.17) | copy-start | bytes 1924
  111.8 14.2 %all-to-all-start.2 = ((bf16[8,2,10240]{2,1,0:T(2,128)(2,1)}), bf16[8,2,10240]{2,1,0:T(2,128)(2,1)S(1)}, u32[]{:S(2)}, u32[]{:S(2)}) async-start(bf16[8,2,10240]{2,1,0:T(2,128)(2,1)} %reshape.146), calls=%async_computation.2 | async-start | bytes 655360 | tf_op jit(solution)/shard_map/all_to_all | solution.py:101
  116.0 12.5 %copy-start.3 = (bf16[320,320]{1,0:T(8,128)(2,1)S(1)}, bf16[320,320]{1,0:T(8,128)(2,1)}, u32[]{:S(2)}) copy-start(bf16[320,320]{1,0:T(8,128)(2,1)} %param.16) | copy-start | bytes 614404
  129.2 20.9 %copy-start.5 = (bf16[320]{0:T(512)(128)(2,1)S(1)}, bf16[320]{0:T(512)(128)(2,1)}, u32[]{:S(2)}) copy-start(bf16[320]{0:T(512)(128)(2,1)} %param.19) | copy-start | bytes 1924
  145.3 5.4 %collective-permute-start.7 = (bf16[4,1,32,320]{3,2,1,0:T(8,128)(2,1)}, bf16[4,1,32,320]{3,2,1,0:T(8,128)(2,1)S(1)}, u32[]{:S(2)}, u32[]{:S(2)}) collective-permute-start(bf16[4,1,32,320]{3,2,1,0:T(8,128)(2,1)} %get-tuple-element.123), channel_id=1, source_target_pairs={{0,1},{1,2},{2,3},{3,4},{4,5},{5,6},{6,7},{8,9},{9,10},{10,11},{11... | collective-permute-start | bytes 245768 | tf_op jit(solution)/shard_map/ppermute | solution.py:37
  147.2 6.3 %collective-permute-start.8 = (bf16[4,1,32,320]{3,2,1,0:T(8,128)(2,1)}, bf16[4,1,32,320]{3,2,1,0:T(8,128)(2,1)}, u32[]{:S(2)}, u32[]{:S(2)}) collective-permute-start(bf16[4,1,32,320]{3,2,1,0:T(8,128)(2,1)} %get-tuple-element.124), channel_id=1, source_target_pairs={{1,0},{2,1},{3,2},{4,3},{5,4},{6,5},{7,6},{9,8},{10,9},{11,10},{12... | collective-permute-start | bytes 245768 | tf_op jit(solution)/shard_map/ppermute | solution.py:38
  154.7 1.6 %copy-start.2 = (bf16[3,3,320,320]{3,2,1,0:T(8,128)(2,1)S(1)}, bf16[3,3,320,320]{3,2,1,0:T(8,128)(2,1)}, u32[]{:S(2)}) copy-start(bf16[3,3,320,320]{3,2,1,0:T(8,128)(2,1)} %param.18) | copy-start | bytes 5529604

commit v2 on v0

v2 whole, which is shorter than its diff:
```python
import math, functools
import jax, jax.numpy as jnp
from jax import lax
from jax.sharding import PartitionSpec as P
from jax.experimental import pallas as pl
from jax.experimental.pallas import tpu as pltpu

HEADS = 8
GROUPS = 32
LANES = 128
PER_TILE = 3
BF = jnp.bfloat16
F32 = jnp.float32


def spread_matrix(channels, head_dim, tiles):
    used = PER_TILE * head_dim
    row = lax.broadcasted_iota(jnp.int32, (channels, tiles * LANES), 0)
    col = lax.broadcasted_iota(jnp.int32, (channels, tiles * LANES), 1)
    inside = col % LANES
    return jnp.where((inside < used) & (row == (col // LANES) * used + inside), 1.0, 0.0).astype(BF)


def dot_nt(a, b):
    return lax.dot_general(a, b, (((1,), (1,)), ((), ())), preferred_element_type=F32)


def dot_tn(a, b):
    return lax.dot_general(a, b, (((0,), (0,)), ((), ())), preferred_element_type=F32)


def dot(a, b):
    return jnp.dot(a, b, preferred_element_type=F32)


def attention_kernel(head_dim, g_ref, n_ref, x_ref, wq_ref, wk_ref, wv_ref, wo_ref, out_ref, sum_ref,
                     wkv_s, wo_s, q_s, k_s, v_s, acc_s, top_s, att_s):
    frames, own, channels = n_ref.shape
    tiles = -(-HEADS // PER_TILE)
    wide = tiles * LANES
    used = PER_TILE * head_dim
    scale = math.log2(math.e) / math.sqrt(head_dim)
    spread = spread_matrix(channels, head_dim, tiles)
    wkv_s[:, :wide] = dot(wk_ref[...], spread).astype(BF)
    wkv_s[:, wide:] = dot(wv_ref[...], spread).astype(BF)
    wo_s[...] = dot_tn(spread, wo_ref[...]).astype(BF)
    wq = dot(wq_ref[...], spread).astype(BF)
    heads_in = [min(PER_TILE, HEADS - t * PER_TILE) for t in range(tiles)]
    lane = lax.broadcasted_iota(jnp.int32, (own, LANES), 1)
    for f in range(frames):
        q = dot(n_ref[f], wq)
        for t in range(tiles):
            part = q[:, t * LANES:(t + 1) * LANES]
            for j in range(heads_in[t]):
                kept = jnp.where((lane >= j * head_dim) & (lane < (j + 1) * head_dim), part, 0.0)
                q_s[f, t, j * own:(j + 1) * own, :] = kept.astype(BF)

    def project(slot):
        rows = 256
        count = g_ref.shape[1] // rows
        inside = lax.broadcasted_iota(jnp.int32, (rows, wide), 1) % LANES
        for i in range(count):
            both = dot(g_ref[slot, i * rows:(i + 1) * rows, :], wkv_s[...])
            k_s[i * rows:(i + 1) * rows, :] = both[:, :wide].astype(BF)
            v_s[i * rows:(i + 1) * rows, :] = jnp.where(inside >= used, 1.0, both[:, wide:]).astype(BF)

    def unit(f, t):
        rows = heads_in[t] * own
        s = dot_nt(q_s[f, t, :rows, :], k_s[:, t * LANES:(t + 1) * LANES])
        top = jnp.max(s, axis=-1, keepdims=True)
        w = jnp.exp2((s - top) * scale).astype(BF)
        return top, dot(w, v_s[:, t * LANES:(t + 1) * LANES]), rows

    def first(f, carry):
        project(f)
        for t in range(tiles):
            top, acc, rows = unit(f, t)
            acc_s[f, t, :rows, :] = acc
            top_s[f, t, :rows, :] = jnp.broadcast_to(top, (rows, LANES))
        return carry

    lax.fori_loop(0, frames, first, 0)
    project(frames)

    def second(f, carry):
        for t in range(tiles):
            top, acc, rows = unit(f, t)
            before = top_s[f, t, :rows, :]
            high = jnp.maximum(before, top)
            acc = acc * jnp.exp2((top - high) * scale) + acc_s[f, t, :rows, :] * jnp.exp2((before - high) * scale)
            acc = acc / acc[:, used:used + 1]
            whole = jnp.zeros((own, LANES), F32)
            for j in range(heads_in[t]):
                whole = jnp.where((lane >= j * head_dim) & (lane < (j + 1) * head_dim),
                                  acc[j * own:(j + 1) * own, :], whole)
            att_s[f, :, t * LANES:(t + 1) * LANES] = whole.astype(BF)
        mixed = dot(att_s[f], wo_s[...])
        updated = (x_ref[f].astype(F32) + mixed).astype(BF)
        out_ref[f] = updated
        wider = updated.astype(F32)
        sum_ref[pl.ds(f, 1), :] = jnp.sum(wider, axis=0, keepdims=True)
        sum_ref[pl.ds(frames + f, 1), :] = jnp.sum(wider * wider, axis=0, keepdims=True)
        return carry

    lax.fori_loop(0, frames, second, 0)


def attention(gathered, normed, x, wq, wk, wv, wo):
    frames, own, channels = normed.shape
    head_dim = channels // HEADS
    tiles = -(-HEADS // PER_TILE)
    wide = tiles * LANES
    keys = gathered.shape[1]
    rows = PER_TILE * own
    vm = pl.BlockSpec(memory_space=pltpu.VMEM)
    return pl.pallas_call(
        functools.partial(attention_kernel, head_dim),
        out_shape=(jax.ShapeDtypeStruct((frames, own, channels), BF),
                   jax.ShapeDtypeStruct((2 * frames, channels), F32)),
        in_specs=[vm] * 7,
        out_specs=(vm, vm),
        scratch_shapes=[
            pltpu.VMEM((channels, 2 * wide), BF),
            pltpu.VMEM((wide, channels), BF),
            pltpu.VMEM((frames, tiles, rows, LANES), BF),
            pltpu.VMEM((keys, wide), BF),
            pltpu.VMEM((keys, wide), BF),
            pltpu.VMEM((frames, tiles, rows, LANES), F32),
            pltpu.VMEM((frames, tiles, rows, LANES), F32),
            pltpu.VMEM((frames, own, wide), BF),
        ],
        compiler_params=pltpu.CompilerParams(vmem_limit_bytes=48 * 1024 * 1024),
    )(gathered, normed, x, wq, wk, wv, wo)


MESH = pl.DeviceIdType.MESH


def normalize(x, gain):
    wide = x.astype(F32)
    centre = wide - jnp.mean(wide, axis=-1, keepdims=True)
    spread = jnp.mean(centre * centre, axis=-1, keepdims=True)
    return (centre * lax.rsqrt(spread + 1e-5) * gain).astype(BF)


def tree_place(b):
    y, q = b % 8, b // 8
    x, h = q // 2, q % 2
    y_depth = jnp.where(y == 0, 0, jnp.where((y == 3) | (y == 6), 1, 2))
    x_depth = jnp.where(x == 0, 0, jnp.where(x == 2, 2, 1))
    parent = jnp.where(
        x > 0,
        jnp.where(x == 3, b - 48, b - 16),
        jnp.where(
            y > 0,
            jnp.where((y == 2) | (y == 5), b + 1, jnp.where((y == 1) | (y == 4), b - 1, b - y)),
            b - 8,
        ),
    )
    edge = x == 0
    children = [
        (edge & (h == 0) & (y == 0), b + 8),
        (edge & ((y == 0) | (y == 3) | (y == 6)), jnp.where(y == 0, b + 3, b - 1)),
        (edge & ((y == 0) | (y == 3)), jnp.where(y == 0, b + 6, b + 1)),
        (edge & (y == 0), b + 1),
        (edge & (y == 0), b + 7),
        (x <= 1, b + 16),
        (edge, b + 48),
    ]
    return h + y_depth + x_depth, parent, children


TREE_DEPTH = 6
TREE_CHILDREN = 7


class Gather:
    def __init__(self, g_ref, n_ref, recv, row_send, tree_send, prev_send):
        self.g, self.n = g_ref, n_ref
        self.recv, self.row_send, self.tree_send, self.prev_send = recv, row_send, tree_send, prev_send
        self.size = lax.axis_size("frame")
        self.chips = lax.axis_size("row") // 2
        self.b = lax.axis_index("frame")
        self.r = lax.axis_index("row")
        self.z, self.c = self.r // 2, self.r % 2
        self.other = self.r + 1 - 2 * self.c
        self.depth, self.parent, children = tree_place(self.b)
        self.children = [(cond & (to < self.size), to) for cond, to in children]
        self.slots = g_ref.shape[0]
        self.lead = self.slots - 1

    def greet(self, everyone):
        barrier = pltpu.get_barrier_semaphore()
        total = jnp.int32(0)

        def hail(cond, b, r):
            @pl.when(cond)
            def _():
                pl.semaphore_signal(barrier, inc=1, device_id=(b, r), device_id_type=MESH)
            return jnp.where(cond, 1, 0)

        b, r, size = self.b, self.r, self.size
        for d in range(1, lax.axis_size("row")):
            to = (r + d) % lax.axis_size("row")
            if everyone:
                total += hail(r >= 0, b, to)
            else:
                total += hail((to == r + 2) | (to == r - 2) | (to == self.other), b, to)
        total += hail(b > 0, b - 1, r)
        total += hail(b < size - 1, b + 1, r)
        total += hail(b > 0, self.parent, r)
        for cond, to in self.children:
            total += hail(cond, to, r)
        pl.semaphore_wait(barrier, total)

    def row_copy(self, s, chip, kind, index):
        to = [self.r + 2, self.r - 2, self.other][kind]
        shard = 2 * chip + self.c
        return pltpu.make_async_remote_copy(
            src_ref=self.g.at[s, shard], dst_ref=self.g.at[s, shard],
            send_sem=self.row_send.at[s, kind, index], recv_sem=self.recv.at[s, shard],
            device_id=(self.b, to), device_id_type=MESH)

    def arrived(self, s, shard):
        pltpu.make_async_remote_copy(
            src_ref=self.g.at[s, shard], dst_ref=self.g.at[s, shard],
            send_sem=self.row_send.at[s, 0, 0], recv_sem=self.recv.at[s, shard],
            device_id=(self.b, self.other), device_id_type=MESH).wait_recv()

    def pass_on(self, s, t, right, left):
        z, last = self.z, self.chips - 1
        if right:
            @pl.when(z < last)
            def _():
                self.row_copy(s, z - t, 0, t).start()
        if left:
            @pl.when(z > 0)
            def _():
                self.row_copy(s, z + t, 1, t).start()
        chip = z - t if right else z + t
        self.row_copy(s, chip, 2, chip).start()

    def step(self, s, t):
        z, last = self.z, self.chips - 1
        if t == 0:
            self.pass_on(s, 0, True, True)
            return

        @pl.when(z - t >= 0)
        def _():
            self.arrived(s, 2 * (z - t) + self.c)
            self.pass_on(s, t, True, False)

        @pl.when(z + t <= last)
        def _():
            self.arrived(s, 2 * (z + t) + self.c)
            self.pass_on(s, t, False, True)

    def finish(self, s):
        for chip in range(self.chips):
            self.arrived(s, 2 * chip + 1 - self.c)

    def drain(self, s):
        z, last = self.z, self.chips - 1
        for t in range(self.chips):
            @pl.when((z - t >= 0) & (z < last))
            def _():
                self.row_copy(s, z - t, 0, t).wait_send()

            @pl.when((z + t <= last) & (z > 0))
            def _():
                self.row_copy(s, z + t, 1, t).wait_send()
            self.row_copy(s, t, 2, t).wait_send()

    def prev_copy(self):
        return pltpu.make_async_remote_copy(
            src_ref=self.n.at[self.n.shape[0] - 1], dst_ref=self.g.at[0, self.r],
            send_sem=self.prev_send, recv_sem=self.recv.at[0, self.r],
            device_id=(self.b + 1, self.r), device_id_type=MESH)

    def prev_start(self):
        @pl.when(self.b < self.size - 1)
        def _():
            self.prev_copy().start()

    def prev_arrived(self):
        @pl.when(self.b > 0)
        def _():
            self.arrived(0, self.r)

    def prev_drain(self):
        @pl.when(self.b < self.size - 1)
        def _():
            self.prev_copy().wait_send()

    def tree_copy(self, index, to):
        return pltpu.make_async_remote_copy(
            src_ref=self.g.at[self.lead, self.r], dst_ref=self.g.at[self.lead, self.r],
            send_sem=self.tree_send.at[index], recv_sem=self.recv.at[self.lead, self.r],
            device_id=(to, self.r), device_id_type=MESH)

    def tree_step(self, level):
        @pl.when(self.depth == level)
        def _():
            if level > 0:
                self.arrived(self.lead, self.r)
            for index, (cond, to) in enumerate(self.children):
                @pl.when(cond)
                def _():
                    self.tree_copy(index, to).start()

    def tree_drain(self):
        for index, (cond, to) in enumerate(self.children):
            @pl.when(cond)
            def _():
                self.tree_copy(index, to).wait_send()


def gather_kernel(x_ref, gain_ref, g_ref, n_ref, recv, row_send, tree_send, prev_send):
    frames = x_ref.shape[0]
    net = Gather(g_ref, n_ref, recv, row_send, tree_send, prev_send)
    net.greet(False)
    gain = gain_ref[...].astype(F32)
    for f in range(frames):
        normed = normalize(x_ref[f], gain)
        n_ref[f] = normed
        if f + 1 < frames:
            g_ref[1 + f, net.r] = normed

    @pl.when(net.b == 0)
    def _():
        g_ref[0, net.r] = n_ref[0]
        g_ref[net.lead, net.r] = n_ref[0]

    net.tree_step(0)
    net.prev_start()
    mine = list(range(1, frames))
    for s in mine:
        net.step(s, 0)
    net.prev_arrived()
    net.step(0, 0)
    order = mine + [0]
    for t in range(1, net.chips):
        for s in order:
            net.step(s, t)
        net.tree_step(t)
    for level in range(net.chips, TREE_DEPTH):
        net.tree_step(level)
    for t in range(net.chips):
        net.step(net.lead, t)
    for s in order + [net.lead]:
        net.finish(s)
    for s in order + [net.lead]:
        net.drain(s)
    net.prev_drain()
    net.tree_drain()


def gather(x, gain):
    frames, own, channels = x.shape
    rows = lax.axis_size("row")
    vm = pl.BlockSpec(memory_space=pltpu.VMEM)
    slots = frames + 1
    return pl.pallas_call(
        gather_kernel,
        out_shape=(jax.ShapeDtypeStruct((slots, rows, own, channels), BF),
                   jax.ShapeDtypeStruct((frames, own, channels), BF)),
        in_specs=[vm] * 2,
        out_specs=(vm, vm),
        scratch_shapes=[
            pltpu.SemaphoreType.DMA((slots, rows)),
            pltpu.SemaphoreType.DMA((slots, 3, rows // 2)),
            pltpu.SemaphoreType.DMA((TREE_CHILDREN,)),
            pltpu.SemaphoreType.DMA,
        ],
        compiler_params=pltpu.CompilerParams(
            collective_id=0, has_side_effects=True, vmem_limit_bytes=32 * 1024 * 1024),
    )(x, gain)


class Tail:
    def __init__(self, u_ref, all_ref, halo_ref, sum_send, sum_recv, halo_send, halo_recv):
        self.u, self.all, self.halo = u_ref, all_ref, halo_ref
        self.sum_send, self.sum_recv, self.halo_send, self.halo_recv = sum_send, sum_recv, halo_send, halo_recv
        self.rows = lax.axis_size("row")
        self.b, self.r = lax.axis_index("frame"), lax.axis_index("row")

    def peer(self, d):
        return (self.r + d) % self.rows

    def greet(self):
        barrier = pltpu.get_barrier_semaphore()
        for d in range(1, self.rows):
            pl.semaphore_signal(barrier, inc=1, device_id=(self.b, self.peer(d)), device_id_type=MESH)
        pl.semaphore_wait(barrier, self.rows - 1)

    def sum_copy(self, d):
        return pltpu.make_async_remote_copy(
            src_ref=self.all.at[0], dst_ref=self.all.at[d],
            send_sem=self.sum_send.at[d], recv_sem=self.sum_recv.at[d],
            device_id=(self.b, self.peer(d)), device_id_type=MESH)

    def halo_copy(self, side):
        width, own = self.halo.shape[2], self.u.shape[1]
        to = self.r + 1 if side == 0 else self.r - 1
        start = own - width if side == 0 else 0
        return pltpu.make_async_remote_copy(
            src_ref=self.u.at[:, pl.ds(start, width), :], dst_ref=self.halo.at[side],
            send_sem=self.halo_send.at[side], recv_sem=self.halo_recv.at[side],
            device_id=(self.b, to), device_id_type=MESH)

    def start(self):
        last = self.rows - 1

        @pl.when(self.r < last)
        def _():
            self.halo_copy(0).start()

        @pl.when(self.r > 0)
        def _():
            self.halo_copy(1).start()
        for d in range(1, self.rows):
            self.sum_copy(d).start()

    def wait(self):
        last = self.rows - 1
        for d in range(1, self.rows):
            self.sum_copy(d).wait()

        @pl.when(self.r > 0)
        def _():
            self.halo_copy(0).wait_recv()

        @pl.when(self.r < last)
        def _():
            self.halo_copy(1).wait_recv()

        @pl.when(self.r < last)
        def _():
            self.halo_copy(0).wait_send()

        @pl.when(self.r > 0)
        def _():
            self.halo_copy(1).wait_send()


def convolve(tail, gain_ref, w_ref, bias_ref, out_ref, act_s):
    u_ref, all_ref, halo_ref = tail.u, tail.all, tail.halo
    frames, own, channels = u_ref.shape
    width = halo_ref.shape[2]
    group = channels // GROUPS
    total = all_ref[0]
    for d in range(1, tail.rows):
        total = total + all_ref[d]
    same = (lax.broadcasted_iota(jnp.int32, (channels, channels), 0) // group
            == lax.broadcasted_iota(jnp.int32, (channels, channels), 1) // group)
    grouped = jnp.dot(total, jnp.where(same, 1.0, 0.0), preferred_element_type=F32,
                      precision=lax.Precision.HIGHEST)
    counted = own * tail.rows * group
    mean = grouped[:frames] / counted
    var = grouped[frames:] / counted - mean * mean
    scale = lax.rsqrt(var + 1e-5)
    gain = gain_ref[...].astype(F32)
    tall = own + 2 * width
    place = lax.broadcasted_iota(jnp.int32, (tall, channels), 0)
    column = place % width
    real = ((place >= width) | (tail.r > 0)) & ((place < width + own) | (tail.r < tail.rows - 1))
    for f in range(frames):
        u = jnp.concatenate([halo_ref[0, f], u_ref[f], halo_ref[1, f]], axis=0).astype(F32)
        v = (u - mean[f:f + 1]) * scale[f:f + 1] * gain
        v = jnp.where(real, v / (1.0 + jnp.exp(-v)), 0.0)
        act_s[0, f] = jnp.where(column == 0, 0.0, pltpu.roll(v, 1, 0)).astype(BF)
        act_s[1, f] = v.astype(BF)
        act_s[2, f] = jnp.where(column == width - 1, 0.0, pltpu.roll(v, tall - 1, 0)).astype(BF)
    total = u_ref[...].reshape(frames * own, channels).astype(F32) + bias_ref[...].astype(F32)
    summed = None
    for a in range(3):
        for b in range(3):
            window = act_s[b, :, a * width:a * width + own, :].reshape(frames * own, channels)
            part = dot(window, w_ref[a, b])
            summed = part if summed is None else summed + part
    out_ref[...] = (total + summed).astype(BF).reshape(frames, own, channels)


def tail_kernel(u_ref, sum_ref, gain_ref, w_ref, bias_ref, out_ref, all_s, halo_s, act_s,
                sum_send, sum_recv, halo_send, halo_recv):
    tail = Tail(u_ref, all_s, halo_s, sum_send, sum_recv, halo_send, halo_recv)
    all_s[0] = sum_ref[...]
    halo_r = tail.r

    @pl.when(halo_r == 0)
    def _():
        halo_s[0] = jnp.zeros(halo_s.shape[1:], BF)

    @pl.when(halo_r == tail.rows - 1)
    def _():
        halo_s[1] = jnp.zeros(halo_s.shape[1:], BF)
    tail.greet()
    tail.start()
    tail.wait()
    convolve(tail, gain_ref, w_ref, bias_ref, out_ref, act_s)


def finish(updated, sums, gain, conv, bias, width):
    frames, own, channels = updated.shape
    rows = lax.axis_size("row")
    vm = pl.BlockSpec(memory_space=pltpu.VMEM)
    return pl.pallas_call(
        tail_kernel,
        out_shape=jax.ShapeDtypeStruct((frames, own, channels), BF),
        in_specs=[vm] * 5,
        out_specs=vm,
        scratch_shapes=[
            pltpu.VMEM((rows, 2 * frames, channels), F32),
            pltpu.VMEM((2, frames, width, channels), BF),
            pltpu.VMEM((3, frames, own + 2 * width, channels), BF),
            pltpu.SemaphoreType.DMA((rows,)),
            pltpu.SemaphoreType.DMA((rows,)),
            pltpu.SemaphoreType.DMA((2,)),
            pltpu.SemaphoreType.DMA((2,)),
        ],
        compiler_params=pltpu.CompilerParams(
            collective_id=1, has_side_effects=True, vmem_limit_bytes=32 * 1024 * 1024),
    )(updated, sums, gain, conv, bias)


def body(latents, ln_gain, q_weight, k_weight, v_weight, o_weight, gn_gain, conv_weight, conv_bias):
    frames, row_count, col_count, channels = latents.shape
    x = latents.reshape(frames, row_count * col_count, channels)
    gathered, normed = gather(x, ln_gain.reshape(1, channels))
    gathered = gathered.reshape(frames + 1, -1, channels)
    updated, sums = attention(gathered, normed, x, q_weight, k_weight, v_weight, o_weight)
    out = finish(updated, sums, gn_gain.reshape(1, channels), conv_weight,
                 conv_bias.reshape(1, channels), col_count)
    return out.reshape(frames, row_count, col_count, channels)


def solution(mesh):
    in_specs = (P("frame", "row", None, None), P(), P(), P(), P(), P(), P(), P(), P())
    out_specs = P("frame", "row", None, None)
    return jax.shard_map(body, mesh=mesh, in_specs=in_specs, out_specs=out_specs, check_vma=False)
```

time: 902 us -> 97.3 us (0.11)
  waiting for transfers between devices: 777 us -> 0 us
  Pallas kernels: 0 us -> 89.5 us
  starting transfers between devices: 48 us -> 0 us
  matrix products: 16.6 us -> 0 us
  other arithmetic: 16.1 us -> 0 us
  blocking collectives: 14.1 us -> 0 us
  between operations: 13.9 us -> 0.08 us
    psum x1 -> x0, waiting for transfers between devices: 742 us -> none  [spread_2(): return lax.psum(kept, axis)]
    pallas_call x0 -> x3, Pallas kernels: none -> 89.5 us  [the longest x1 60.7 us: gather(): pl.pallas_call(gather_kernel, out_shape=(jax.ShapeDtypeStruct((slots, row...]
    all_to_all x3 -> x0, starting transfers between devices: 41.5 us -> none  [the longest x1 27.1 us: body(): lax.all_to_all(sent_pairs, 'row', split_axis=3, concat_axis=1, tiled=True)]
    all_to_all x3 -> x0, waiting for transfers between devices: 30.4 us -> none  [the longest x1 20.5 us: body(): lax.all_to_all(sent_pairs, 'row', split_axis=3, concat_axis=1, tiled=True)]
    dot_general x20 -> x0, matrix products: 16.6 us -> none  [the longest x4 6.14 us: single(): jnp.einsum('hqk,khd->qhd', raised.astype(jnp.bfloat16), all_values, prefe...]
    psum x1 -> x0, blocking collectives: 14.1 us -> none  [body(): group_sum, group_square = lax.psum((sum_parts, square_parts), 'row')]
    reduce_sum x7 -> x0, other arithmetic: 10.5 us -> none  [the longest x4 7.73 us: single(): totals = jnp.sum(raised, axis=-1)]
  transfers between devices with their start and end apart: 7 -> 0, of which waited for: 5 -> 0; matrix products, arithmetic and copies ran while one was open for 1% -> 0% of each run, Pallas kernels for 0% -> 0%
where the time goes in v2:
time: 97.3 us; the launch traced here: 96.9 us
  Pallas kernels  89.5 us (92%)
  local copies, waits for them, and re-layouts  7.36 us (8%)
    pallas_call x1, Pallas kernels, gather(): pl.pallas_call(gather_kernel, out_shape=(jax.ShapeDtypeStruct((slots, row...  60.7 us
    pallas_call x1, Pallas kernels, attention(): pl.pallas_call(functools.partial(attention_kernel, head_dim), out_shape=(...  18.3 us
    pallas_call x1, Pallas kernels, finish(): pl.pallas_call(tail_kernel, out_shape=jax.ShapeDtypeStruct((frames, own,...  10.4 us
    unnamed x19, local copies, waits for them, and re-layouts  6.52 us

profile of v2, /device:TPU:1, one launch (start us, length us, event | category | flops | bytes accessed | tf_op | source)
XLA Modules:
  0.0 96.9 jit_solution(13489738217778796197)
XLA Ops:
  0.0 0.0 copy-start
  0.0 0.8 reshape.19.gain_ref
  0.8 0.0 copy-start.1
  0.8 1.0 %copy-done.1 = bf16[4,4,32,320]{3,2,1,0:T(8,128)(2,1)S(1)} copy-done((bf16[4,4,32,320]{3,2,1,0:T(8,128)(2,1)S(1)}, bf16[4,4,32,320]{3,2,1,0:T(8,128)(2,1)}, u32[]{:S(2)}) %copy-start.1) | copy-done | bytes 327704
  1.8 60.7 %shard_map.91 = (bf16[5,8,128,320]{3,2,1,0:T(8,128)(2,1)S(1)}, bf16[4,128,320]{2,1,0:T(8,128)(2,1)S(1)}) custom-call(bf16[4,128,320]{2,1,0:T(8,128)(2,1)S(1)} %bitcast.4, bf16[1,320]{1,0:T(2,128)(2,1)S(1)} %reshape.19.gain_ref), custom_call_target="tpu_custom_call" | custom-call | tf_op jit(solution)/shard_map/pallas_call | solution.py:364
  62.6 0.0 copy-start.2
  62.6 1.0 %copy-done.2 = bf16[4,4,32,320]{3,2,1,0:T(8,128)(2,1)S(1)} copy-done((bf16[4,4,32,320]{3,2,1,0:T(8,128)(2,1)S(1)}, bf16[4,4,32,320]{3,2,1,0:T(8,128)(2,1)}, u32[]{:S(2)}) %copy-start.2) | copy-done | bytes 327704
  63.6 0.0 copy-start.3
  63.6 0.9 copy-done.3
  64.5 0.0 copy-start.4
  64.5 0.9 copy-done.4
  65.5 0.0 copy-start.5
  65.5 0.9 copy-done.5
  66.4 0.0 copy-start.6
  66.4 0.9 copy-done.6
  67.3 0.0 copy-start.7
  67.3 0.0 copy-start.8
  67.3 18.3 %shard_map.92 = (bf16[4,128,320]{2,1,0:T(8,128)(2,1)S(1)}, f32[8,320]{1,0:T(8,128)S(1)}) custom-call(bf16[5,1024,320]{2,1,0:T(8,128)(2,1)S(1)} %bitcast.3, bf16[4,128,320]{2,1,0:T(8,128)(2,1)S(1)} %get-tuple-element.10.n_ref, bf16[4,128,320]{2,1,0:T(8,128)(2,1)S(1)} %bitcast.5, bf16[320,320]{1,0:T(8,128)(2,1)S(1)} %copy-done.3, ...), custom_call_target="tpu_custom_call" | custom-call | tf_op jit(solution)/shard_map/pallas_call | solution.py:116
  85.7 0.0 copy-done.7
  85.7 0.0 copy-done.8
  85.7 0.0 copy-done
  85.7 10.4 %shard_map.93 = bf16[4,128,320]{2,1,0:T(8,128)(2,1)S(1)} custom-call(bf16[4,128,320]{2,1,0:T(8,128)(2,1)S(1)} %get-tuple-element.11.u_ref, f32[8,320]{1,0:T(8,128)S(1)} %get-tuple-element.12.sum_ref, bf16[1,320]{1,0:T(2,128)(2,1)S(1)} %reshape.21.gain_ref, bf16[3,3,320,320]{3,2,1,0:T(8,128)(2,1)S(1)} %copy-done, bf16[1,320]{1,0:T(2,128)(2,1)S(1)} %reshape.22.bias_ref), custom_call_target="tpu_custom_call" | custom-call | tf_op jit(solution)/shard_map/pallas_call | solution.py:508
  96.2 0.7 copy.11
  (2 shorter events, 0.0 us)
Async XLA Ops:
  0.0 85.7 %copy-start = (bf16[3,3,320,320]{3,2,1,0:T(8,128)(2,1)S(1)}, bf16[3,3,320,320]{3,2,1,0:T(8,128)(2,1)}, u32[]{:S(2)}) copy-start(bf16[3,3,320,320]{3,2,1,0:T(8,128)(2,1)} %w_ref.1) | copy-start | bytes 5529604
  0.8 1.0 %copy-start.1 = (bf16[4,4,32,320]{3,2,1,0:T(8,128)(2,1)S(1)}, bf16[4,4,32,320]{3,2,1,0:T(8,128)(2,1)}, u32[]{:S(2)}) copy-start(bf16[4,4,32,320]{3,2,1,0:T(8,128)(2,1)} %param.9) | copy-start | bytes 983044
  62.6 1.0 %copy-start.2 = (bf16[4,4,32,320]{3,2,1,0:T(8,128)(2,1)S(1)}, bf16[4,4,32,320]{3,2,1,0:T(8,128)(2,1)}, u32[]{:S(2)}) copy-start(bf16[4,4,32,320]{3,2,1,0:T(8,128)(2,1)} %param.9) | copy-start | bytes 983044
  63.6 0.9 copy-start.3
  64.5 0.9 copy-start.4
  65.5 0.9 copy-start.5
  66.4 0.9 copy-start.6
  67.3 18.3 %copy-start.7 = (bf16[320]{0:T(512)(128)(2,1)S(1)}, bf16[320]{0:T(512)(128)(2,1)}, u32[]{:S(2)}) copy-start(bf16[320]{0:T(512)(128)(2,1)} %param.15) | copy-start | bytes 1924
  67.3 18.3 %copy-start.8 = (bf16[320]{0:T(512)(128)(2,1)S(1)}, bf16[320]{0:T(512)(128)(2,1)}, u32[]{:S(2)}) copy-start(bf16[320]{0:T(512)(128)(2,1)} %param.17) | copy-start | bytes 1924

commit v3 on v0

v3 whole, which is shorter than its diff:
```python
import functools
import math

import jax
import jax.numpy as jnp
from jax import lax
from jax.experimental import pallas as pl
from jax.experimental.pallas import tpu as pltpu
from jax.sharding import PartitionSpec as P

HEADS = 8
GROUPS = 32
LANES = 128
PER_TILE = 3
BF = jnp.bfloat16
F32 = jnp.float32
MESH = pl.DeviceIdType.MESH
TREE_DEPTH = 6
TREE_CHILDREN = 7


def dot(a, b):
    return jnp.dot(a, b, preferred_element_type=F32)


def dot_nt(a, b):
    return lax.dot_general(a, b, (((1,), (1,)), ((), ())), preferred_element_type=F32)


def dot_tn(a, b):
    return lax.dot_general(a, b, (((0,), (0,)), ((), ())), preferred_element_type=F32)


def one_hot(rows, columns, test):
    row = lax.broadcasted_iota(jnp.int32, (rows, columns), 0)
    col = lax.broadcasted_iota(jnp.int32, (rows, columns), 1)
    return jnp.where(test(row, col), 1.0, 0.0).astype(BF)


def normalize(x, gain):
    wide = x.astype(F32)
    centre = wide - jnp.mean(wide, axis=-1, keepdims=True)
    spread = jnp.mean(centre * centre, axis=-1, keepdims=True)
    return (centre * lax.rsqrt(spread + 1e-5) * gain).astype(BF)


def tree_place(b):
    y, q = b % 8, b // 8
    x, h = q // 2, q % 2
    y_depth = jnp.where(y == 0, 0, jnp.where((y == 3) | (y == 6), 1, 2))
    x_depth = jnp.where(x == 0, 0, jnp.where(x == 2, 2, 1))
    y_parent = jnp.where((y == 2) | (y == 5), b + 1, jnp.where((y == 1) | (y == 4), b - 1, b - y))
    parent = jnp.where(x > 0, jnp.where(x == 3, b - 48, b - 16), jnp.where(y > 0, y_parent, b - 8))
    y_index = jnp.where((y == 1) | (y == 7), jnp.where(y == 1, 3, 4), jnp.where((y == 6) | (y == 4), 2, 1))
    index = jnp.where(x > 0, jnp.where(x == 3, 6, 5), jnp.where(y > 0, y_index, 0))
    edge = x == 0
    children = [
        (edge & (h == 0) & (y == 0), b + 8),
        (edge & ((y == 0) | (y == 3) | (y == 6)), jnp.where(y == 0, b + 3, b - 1)),
        (edge & ((y == 0) | (y == 3)), jnp.where(y == 0, b + 6, b + 1)),
        (edge & (y == 0), b + 1),
        (edge & (y == 0), b + 7),
        (x <= 1, b + 16),
        (edge, b + 48),
    ]
    return h + y_depth + x_depth, parent, index, children


TREE_ORDER = (1, 2, 3, 4, 5, 6, 0)


class Net:
    def __init__(self, g_ref, last_ref, u_ref, all_ref, halo_ref, sems):
        self.g, self.last, self.u, self.all, self.halo = g_ref, last_ref, u_ref, all_ref, halo_ref
        (self.recv, self.row_send, self.tree_send, self.prev_send, self.tree_ready, self.prev_ready,
         self.sum_send, self.sum_recv, self.halo_send, self.halo_recv) = sems
        self.size = lax.axis_size("frame")
        self.rows = lax.axis_size("row")
        self.chips = self.rows // 2
        self.b = lax.axis_index("frame")
        self.r = lax.axis_index("row")
        self.z, self.c = self.r // 2, self.r % 2
        self.other = self.r + 1 - 2 * self.c
        self.depth, self.parent, self.index, children = tree_place(self.b)
        self.children = [(cond & (to < self.size), to) for cond, to in children]
        self.lead = g_ref.shape[0] - 1

    def peer(self, d):
        return (self.r + d) % self.rows

    def hail(self):
        barrier = pltpu.get_barrier_semaphore()

        def signal(cond, b, r):
            @pl.when(cond)
            def _():
                pl.semaphore_signal(barrier, inc=1, device_id=(b, r), device_id_type=MESH)

        for d in range(1, self.rows):
            pl.semaphore_signal(barrier, inc=1, device_id=(self.b, self.peer(d)), device_id_type=MESH)
        signal(self.b < self.size - 1, self.b + 1, self.r)
        for cond, to in self.children:
            signal(cond, to, self.r)

    def greet(self):
        barrier = pltpu.get_barrier_semaphore()
        pl.semaphore_wait(barrier, self.rows - 1 + jnp.where(self.b > 0, 2, 0))

        @pl.when(self.b > 0)
        def _():
            pl.semaphore_signal(self.prev_ready, inc=1, device_id=(self.b - 1, self.r), device_id_type=MESH)
            pl.semaphore_signal(self.tree_ready.at[self.index], inc=1, device_id=(self.parent, self.r),
                                device_id_type=MESH)

    def row_copy(self, s, chip, kind, index):
        to = [self.r + 2, self.r - 2, self.other][kind]
        shard = 2 * chip + self.c
        return pltpu.make_async_remote_copy(
            src_ref=self.g.at[s, shard], dst_ref=self.g.at[s, shard],
            send_sem=self.row_send.at[s, kind, index], recv_sem=self.recv.at[s, shard],
            device_id=(self.b, to), device_id_type=MESH)

    def arrived(self, s, shard):
        pltpu.make_async_remote_copy(
            src_ref=self.g.at[s, shard], dst_ref=self.g.at[s, shard],
            send_sem=self.row_send.at[s, 0, 0], recv_sem=self.recv.at[s, shard],
            device_id=(self.b, self.other), device_id_type=MESH).wait_recv()

    def pass_on(self, s, t, right, left):
        z, last = self.z, self.chips - 1
        if right:
            @pl.when(z < last)
            def _():
                self.row_copy(s, z - t, 0, t).start()
        if left:
            @pl.when(z > 0)
            def _():
                self.row_copy(s, z + t, 1, t).start()
        chip = z - t if right else z + t
        self.row_copy(s, chip, 2, chip).start()

    def step(self, s, t):
        z, last = self.z, self.chips - 1
        if t == 0:
            self.pass_on(s, 0, True, True)
            return

        @pl.when(z - t >= 0)
        def _():
            self.arrived(s, 2 * (z - t) + self.c)
            self.pass_on(s, t, True, False)

        @pl.when(z + t <= last)
        def _():
            self.arrived(s, 2 * (z + t) + self.c)
            self.pass_on(s, t, False, True)

    def finish(self, s):
        for chip in range(self.chips):
            self.arrived(s, 2 * chip + 1 - self.c)

    def drain(self, s):
        z, last = self.z, self.chips - 1
        for t in range(self.chips):
            @pl.when((z - t >= 0) & (z < last))
            def _():
                self.row_copy(s, z - t, 0, t).wait_send()

            @pl.when((z + t <= last) & (z > 0))
            def _():
                self.row_copy(s, z + t, 1, t).wait_send()
            self.row_copy(s, t, 2, t).wait_send()

    def prev_copy(self):
        return pltpu.make_async_remote_copy(
            src_ref=self.last, dst_ref=self.g.at[0, self.r],
            send_sem=self.prev_send, recv_sem=self.recv.at[0, self.r],
            device_id=(self.b + 1, self.r), device_id_type=MESH)

    def prev_start(self):
        @pl.when(self.b < self.size - 1)
        def _():
            pl.semaphore_wait(self.prev_ready, 1)
            self.prev_copy().start()

    def prev_arrived(self):
        @pl.when(self.b > 0)
        def _():
            self.arrived(0, self.r)

    def prev_drain(self):
        @pl.when(self.b < self.size - 1)
        def _():
            self.prev_copy().wait_send()

    def tree_copy(self, index, to):
        return pltpu.make_async_remote_copy(
            src_ref=self.g.at[self.lead, self.r], dst_ref=self.g.at[self.lead, self.r],
            send_sem=self.tree_send.at[index], recv_sem=self.recv.at[self.lead, self.r],
            device_id=(to, self.r), device_id_type=MESH)

    def tree_step(self, level):
        @pl.when(self.depth == level)
        def _():
            if level > 0:
                self.arrived(self.lead, self.r)
            for index in TREE_ORDER[:-1]:
                cond, to = self.children[index]

                @pl.when(cond)
                def _():
                    pl.semaphore_wait(self.tree_ready.at[index], 1)
                    self.tree_copy(index, to).start()

    def root_step(self):
        cond, to = self.children[0]

        @pl.when(cond)
        def _():
            pl.semaphore_wait(self.tree_ready.at[0], 1)
            self.tree_copy(0, to).start()

    def tree_drain(self):
        for index, (cond, to) in enumerate(self.children):
            @pl.when(cond)
            def _():
                self.tree_copy(index, to).wait_send()

    def sum_copy(self, f, d):
        return pltpu.make_async_remote_copy(
            src_ref=self.all.at[0, f], dst_ref=self.all.at[d, f],
            send_sem=self.sum_send.at[f, d], recv_sem=self.sum_recv.at[f, d],
            device_id=(self.b, self.peer(d)), device_id_type=MESH)

    def halo_copy(self, f, side):
        width, own = self.halo.shape[2], self.u.shape[1]
        to = self.r + 1 if side == 0 else self.r - 1
        start = own - width if side == 0 else 0
        return pltpu.make_async_remote_copy(
            src_ref=self.u.at[f, pl.ds(start, width), :], dst_ref=self.halo.at[side, f],
            send_sem=self.halo_send.at[f, side], recv_sem=self.halo_recv.at[f, side],
            device_id=(self.b, to), device_id_type=MESH)

    def edge_start(self, f):
        for d in range(1, self.rows):
            self.sum_copy(f, d).start()

        @pl.when(self.r < self.rows - 1)
        def _():
            self.halo_copy(f, 0).start()

        @pl.when(self.r > 0)
        def _():
            self.halo_copy(f, 1).start()

    def edge_wait(self, f):
        for d in range(1, self.rows):
            self.sum_copy(f, d).wait_recv()

        @pl.when(self.r > 0)
        def _():
            self.halo_copy(f, 0).wait_recv()

        @pl.when(self.r < self.rows - 1)
        def _():
            self.halo_copy(f, 1).wait_recv()

    def edge_drain(self, f):
        for d in range(1, self.rows):
            self.sum_copy(f, d).wait_send()

        @pl.when(self.r < self.rows - 1)
        def _():
            self.halo_copy(f, 0).wait_send()

        @pl.when(self.r > 0)
        def _():
            self.halo_copy(f, 1).wait_send()


def block_kernel(head_dim, width, x_hbm, ln_hbm, wq_hbm, wk_hbm, wv_hbm, wo_hbm, gn_hbm, conv_hbm, bias_hbm,
                 out_ref, x_s, ln_s, gn_s, bias_s, w_s, conv_s, n_s, g_s, last_s, wkv_s, wo_s, q_s, k_s, v_s,
                 acc_s, top_s, att_s, u_s, all_s, halo_s, act_s, load, *sems):
    frames, own, channels = x_s.shape
    half = own // 2
    tiles = -(-HEADS // PER_TILE)
    wide = tiles * LANES
    used = PER_TILE * head_dim
    cut = (channels // LANES) * LANES
    scale = math.log2(math.e) / math.sqrt(head_dim)
    net = Net(g_s, last_s, u_s, all_s, halo_s, sems)
    lead = net.lead

    loads = [(x_hbm, x_s), (ln_hbm, ln_s), (wq_hbm, w_s.at[0]), (wk_hbm, w_s.at[1]),
             (wv_hbm, w_s.at[2]), (wo_hbm, w_s.at[3]), (gn_hbm, gn_s), (bias_hbm, bias_s),
             (conv_hbm, conv_s)]
    copies = [pltpu.make_async_copy(a, b, load.at[i]) for i, (a, b) in enumerate(loads)]
    for copy in copies:
        copy.start()
    net.hail()

    heads_in = [min(PER_TILE, HEADS - t * PER_TILE) for t in range(tiles)]
    lane = lax.broadcasted_iota(jnp.int32, (own, LANES), 1)
    low = one_hot(channels, 2 * channels, lambda i, j: i == j)
    high = one_hot(channels, 2 * channels, lambda i, j: i + channels == j)
    copies[0].wait()
    copies[1].wait()
    gain = ln_s[...].astype(F32).reshape(1, channels)

    def norm(f):
        normed = normalize(x_s[f], gain)
        n_s[f] = normed
        packed = (dot(normed[:half], low) + dot(normed[half:], high)).astype(BF)
        if f + 1 < frames:
            g_s[1 + f, net.r] = packed
        else:
            last_s[...] = packed
        if f == 0:
            @pl.when(net.b == 0)
            def _():
                g_s[0, net.r] = packed
                g_s[lead, net.r] = packed

    @pl.when(net.r == 0)
    def _():
        halo_s[0] = jnp.zeros(halo_s.shape[1:], BF)

    @pl.when(net.r == net.rows - 1)
    def _():
        halo_s[1] = jnp.zeros(halo_s.shape[1:], BF)

    norm(0)
    net.greet()
    net.step(1, 0)
    net.tree_step(0)
    norm(1)
    norm(frames - 1)
    norm(2)
    net.step(1, 1)
    net.step(2, 0)
    net.prev_start()

    for i in range(2, 6):
        copies[i].wait()
    spread = one_hot(channels, wide,
                     lambda i, j: (j % LANES < used) & (i == (j // LANES) * used + j % LANES))
    wq = dot(w_s[0], spread).astype(BF)
    wkv_s[...] = jnp.zeros(wkv_s.shape, BF)
    for i in range(2):
        part = dot(w_s[1 + i], spread).astype(BF)
        wkv_s[0, :channels, i * wide:(i + 1) * wide] = part
        wkv_s[1, channels - cut:2 * channels - cut, i * wide:(i + 1) * wide] = part
    wo_s[...] = dot_tn(spread, w_s[3]).astype(BF)
    net.step(1, 2)
    net.root_step()
    net.tree_step(1)
    net.step(2, 1)
    net.step(1, 3)
    for f in range(frames):
        q = dot(n_s[f], wq)
        for t in range(tiles):
            part = q[:, t * LANES:(t + 1) * LANES]
            for j in range(heads_in[t]):
                kept = jnp.where((lane >= j * head_dim) & (lane < (j + 1) * head_dim), part, 0.0)
                q_s[f, t, j * own:(j + 1) * own, :] = kept.astype(BF)

    def project(slot):
        shards = 4
        rows = shards * half
        count = g_s.shape[1] // shards
        inside = lax.broadcasted_iota(jnp.int32, (rows, wide), 1) % LANES
        for i in range(count):
            packed = g_s[slot, i * shards:(i + 1) * shards].reshape(rows, 2 * channels)
            for side in range(2):
                view = packed[:, side * cut:side * cut + wide]
                both = dot(view, wkv_s[side])
                at = (2 * i + side) * rows
                k_s[at:at + rows, :] = both[:, :wide].astype(BF)
                v_s[at:at + rows, :] = jnp.where(inside >= used, 1.0, both[:, wide:]).astype(BF)

    def unit(f, t):
        rows = heads_in[t] * own
        s = dot_nt(q_s[f, t, :rows, :], k_s[:, t * LANES:(t + 1) * LANES])
        top = jnp.max(s, axis=-1, keepdims=True)
        w = jnp.exp2((s - top) * scale).astype(BF)
        return top, dot(w, v_s[:, t * LANES:(t + 1) * LANES]), rows

    def first(f, t):
        top, acc, rows = unit(f, t)
        acc_s[f, t, :rows, :] = acc
        top_s[f, t, :rows, :] = jnp.broadcast_to(top, (rows, LANES))

    def second(f, carry):
        for t in range(tiles):
            top, acc, rows = unit(f, t)
            before = top_s[f, t, :rows, :]
            most = jnp.maximum(before, top)
            acc = acc * jnp.exp2((top - most) * scale) + acc_s[f, t, :rows, :] * jnp.exp2((before - most) * scale)
            acc = acc / acc[:, used:used + 1]
            whole = jnp.zeros((own, LANES), F32)
            for j in range(heads_in[t]):
                whole = jnp.where((lane >= j * head_dim) & (lane < (j + 1) * head_dim),
                                  acc[j * own:(j + 1) * own, :], whole)
            att_s[:, t * LANES:(t + 1) * LANES] = whole.astype(BF)
        updated = (x_s[f].astype(F32) + dot(att_s[...], wo_s[...])).astype(BF)
        u_s[f] = updated
        wider = updated.astype(F32)
        all_s[0, f, 0:1, :] = jnp.sum(wider, axis=0, keepdims=True)
        all_s[0, f, 1:2, :] = jnp.sum(wider * wider, axis=0, keepdims=True)
        net.edge_start(f)
        return carry

    net.tree_step(2)
    net.finish(1)
    project(1)
    net.step(2, 2)
    net.step(3, 0)
    net.tree_step(3)
    first(1, 0)
    net.step(3, 1)
    first(1, 1)
    net.tree_step(4)
    net.step(2, 3)
    first(1, 2)
    net.tree_step(5)
    net.step(lead, 0)
    net.finish(2)
    project(2)
    net.step(3, 2)
    first(2, 0)
    net.step(lead, 1)
    first(2, 1)
    net.step(3, 3)
    net.prev_arrived()
    net.step(0, 0)
    first(2, 2)
    net.finish(3)
    project(3)
    net.step(lead, 2)
    first(3, 0)
    net.step(0, 1)
    first(3, 1)
    net.step(lead, 3)
    first(3, 2)
    net.step(0, 2)
    net.finish(lead)
    project(lead)
    first(0, 0)
    first(0, 1)
    first(0, 2)

    def rest(f, carry):
        @pl.when(f == 1)
        def _():
            net.step(0, 3)
        return second(f, carry)

    lax.fori_loop(1, frames, rest, 0)
    net.finish(0)
    project(0)
    second(0, 0)

    for i in range(6, len(copies)):
        copies[i].wait()
    gn_gain = gn_s[...].astype(F32).reshape(1, channels)
    bias = bias_s[...].astype(F32).reshape(1, channels)
    group = channels // GROUPS
    same = (lax.broadcasted_iota(jnp.int32, (channels, channels), 0) // group
            == lax.broadcasted_iota(jnp.int32, (channels, channels), 1) // group)
    same = jnp.where(same, 1.0, 0.0)
    tall = own + 2 * width
    place = lax.broadcasted_iota(jnp.int32, (tall, channels), 0)
    column = place % width
    real = ((place >= width) | (net.r > 0)) & ((place < width + own) | (net.r < net.rows - 1))
    counted = own * net.rows * group

    def convolve(start, count):
        for f in range(start, start + count):
            net.edge_wait(f)
            total = all_s[0, f]
            for d in range(1, net.rows):
                total = total + all_s[d, f]
            grouped = jnp.dot(jnp.concatenate([total] * 4, axis=0), same, preferred_element_type=F32,
                              precision=lax.Precision.HIGHEST)
            mean = grouped[0:1] / counted
            var = grouped[1:2] / counted - mean * mean
            u = jnp.concatenate([halo_s[0, f], u_s[f], halo_s[1, f]], axis=0).astype(F32)
            v = (u - mean) * lax.rsqrt(var + 1e-5) * gn_gain
            v = jnp.where(real, v / (1.0 + jnp.exp(-v)), 0.0)
            act_s[0, f] = jnp.where(column == 0, 0.0, pltpu.roll(v, 1, 0)).astype(BF)
            act_s[1, f] = v.astype(BF)
            act_s[2, f] = jnp.where(column == width - 1, 0.0, pltpu.roll(v, tall - 1, 0)).astype(BF)
        rows = count * own
        summed = u_s[start:start + count].reshape(rows, channels).astype(F32) + bias
        for a in range(3):
            for b in range(3):
                window = act_s[b, start:start + count, a * width:a * width + own, :].reshape(rows, channels)
                summed = summed + dot(window, conv_s[a, b])
        out_ref[start:start + count] = summed.astype(BF).reshape(count, own, channels)

    convolve(1, frames - 1)
    convolve(0, 1)

    for s in range(lead + 1):
        net.drain(s)
    net.prev_drain()
    net.tree_drain()
    for f in range(frames):
        net.edge_drain(f)


def body(latents, ln_gain, q_weight, k_weight, v_weight, o_weight, gn_gain, conv_weight, conv_bias):
    frames, row_count, col_count, channels = latents.shape
    own = row_count * col_count
    head_dim = channels // HEADS
    tiles = -(-HEADS // PER_TILE)
    wide = tiles * LANES
    rows = lax.axis_size("row")
    slots = frames + 1
    keys = rows * own
    hbm = pl.BlockSpec(memory_space=pl.ANY)
    dma = pltpu.SemaphoreType.DMA
    out = pl.pallas_call(
        functools.partial(block_kernel, head_dim, col_count),
        out_shape=jax.ShapeDtypeStruct((frames, own, channels), BF),
        in_specs=[hbm] * 9,
        out_specs=pl.BlockSpec(memory_space=pltpu.VMEM),
        scratch_shapes=[
            pltpu.VMEM((frames, own, channels), BF),
            pltpu.VMEM((channels,), BF),
            pltpu.VMEM((channels,), BF),
            pltpu.VMEM((channels,), BF),
            pltpu.VMEM((4, channels, channels), BF),
            pltpu.VMEM((3, 3, channels, channels), BF),
            pltpu.VMEM((frames, own, channels), BF),
            pltpu.VMEM((slots, rows, own // 2, 2 * channels), BF),
            pltpu.VMEM((own // 2, 2 * channels), BF),
            pltpu.VMEM((2, wide, 2 * wide), BF),
            pltpu.VMEM((wide, channels), BF),
            pltpu.VMEM((frames, tiles, PER_TILE * own, LANES), BF),
            pltpu.VMEM((keys, wide), BF),
            pltpu.VMEM((keys, wide), BF),
            pltpu.VMEM((frames, tiles, PER_TILE * own, LANES), F32),
            pltpu.VMEM((frames, tiles, PER_TILE * own, LANES), F32),
            pltpu.VMEM((own, wide), BF),
            pltpu.VMEM((frames, own, channels), BF),
            pltpu.VMEM((rows, frames, 2, channels), F32),
            pltpu.VMEM((2, frames, col_count, channels), BF),
            pltpu.VMEM((3, frames, own + 2 * col_count, channels), BF),
            dma((9,)),
            dma((slots, rows)),
            dma((slots, 3, rows // 2)),
            dma((TREE_CHILDREN,)),
            dma,
            pltpu.SemaphoreType.REGULAR((TREE_CHILDREN,)),
            pltpu.SemaphoreType.REGULAR,
            dma((frames, rows)),
            dma((frames, rows)),
            dma((frames, 2)),
            dma((frames, 2)),
        ],
        compiler_params=pltpu.CompilerParams(
            collective_id=0, has_side_effects=True, vmem_limit_bytes=56 * 1024 * 1024),
    )(latents.reshape(frames, own, channels), ln_gain, q_weight, k_weight, v_weight,
      o_weight, gn_gain, conv_weight, conv_bias)
    return out.reshape(frames, row_count, col_count, channels)


def solution(mesh):
    in_specs = (P("frame", "row", None, None), P(), P(), P(), P(), P(), P(), P(), P())
    out_specs = P("frame", "row", None, None)
    return jax.shard_map(body, mesh=mesh, in_specs=in_specs, out_specs=out_specs, check_vma=False)
```

time: 902 us -> 71.5 us (0.08)
  waiting for transfers between devices: 777 us -> 0 us
  Pallas kernels: 0 us -> 69.5 us
  starting transfers between devices: 48 us -> 0 us
  matrix products: 16.6 us -> 0 us
  other arithmetic: 16.1 us -> 0 us
  local copies, waits for them, and re-layouts: 15.9 us -> 1.78 us
  blocking collectives: 14.1 us -> 0 us
  between operations: 13.9 us -> 0.01 us
    psum x1 -> x0, waiting for transfers between devices: 742 us -> none  [spread_2(): return lax.psum(kept, axis)]
    pallas_call x0 -> x1, Pallas kernels: none -> 69.5 us  [body(): pl.pallas_call(functools.partial(block_kernel, head_dim, col_count), out_...]
    all_to_all x3 -> x0, starting transfers between devices: 41.5 us -> none  [the longest x1 27.1 us: body(): lax.all_to_all(sent_pairs, 'row', split_axis=3, concat_axis=1, tiled=True)]
    all_to_all x3 -> x0, waiting for transfers between devices: 30.4 us -> none  [the longest x1 20.5 us: body(): lax.all_to_all(sent_pairs, 'row', split_axis=3, concat_axis=1, tiled=True)]
    dot_general x20 -> x0, matrix products: 16.6 us -> none  [the longest x4 6.14 us: single(): jnp.einsum('hqk,khd->qhd', raised.astype(jnp.bfloat16), all_values, prefe...]
    psum x1 -> x0, blocking collectives: 14.1 us -> none  [body(): group_sum, group_square = lax.psum((sum_parts, square_parts), 'row')]
    reduce_sum x7 -> x0, other arithmetic: 10.5 us -> none  [the longest x4 7.73 us: single(): totals = jnp.sum(raised, axis=-1)]
  transfers between devices with their start and end apart: 7 -> 0, of which waited for: 5 -> 0; matrix products, arithmetic and copies ran while one was open for 1% -> 0% of each run, Pallas kernels for 0% -> 0%
where the time goes in v3:
time: 71.5 us; the launch traced here: 71.2 us
  Pallas kernels  69.5 us (97%)
  local copies, waits for them, and re-layouts  1.78 us (2%)
    pallas_call x1, Pallas kernels, body(): pl.pallas_call(functools.partial(block_kernel, head_dim, col_count), out_...  69.5 us
    unnamed x1, local copies, waits for them, and re-layouts  1.78 us

profile of v3, /device:TPU:1, one launch (start us, length us, event | category | flops | bytes accessed | tf_op | source)
XLA Modules:
  0.0 71.2 jit_solution(3073500067728611976)
XLA Ops:
  0.0 69.5 %shard_map.91 = bf16[4,128,320]{2,1,0:T(8,128)(2,1)} custom-call(bf16[4,128,320]{2,1,0:T(8,128)(2,1)} %bitcast.3, bf16[320]{0:T(512)(128)(2,1)} %ln_hbm.1, bf16[320,320]{1,0:T(8,128)(2,1)} %wq_hbm.1, bf16[320,320]{1,0:T(8,128)(2,1)} %wk_hbm.1, bf16[320,320]{1,0:T(8,128)(2,1)} %wv_hbm.1, bf16[320,320]{1,0:T(8,128)(2,1)} %wo_hbm.1, bf16[320]{0:T(512)(128)(2,1)} %gn_hbm.1, ...), custom_call_target="tpu_custom_call" | custom-call | tf_op jit(solution)/shard_map/pallas_call | solution.py:523
  69.5 1.8 %copy.11 = bf16[4,4,32,320]{3,2,1,0:T(8,128)(2,1)} copy(bf16[4,4,32,320]{3,2,1,0:T(8,128)(2,1)} %bitcast.2) | data formatting | bytes 655360

commit v4 on v3

--- a/solution.py
+++ b/solution.py
@@ -15,8 +15,8 @@
 BF = jnp.bfloat16
 F32 = jnp.float32
 MESH = pl.DeviceIdType.MESH
-TREE_DEPTH = 6
-TREE_CHILDREN = 7
+TREE_CHILDREN = 8
+TREE_ORDER = (1, 2, 5, 7, 3, 4, 6)
 
 
 def dot(a, b):
@@ -44,29 +44,36 @@
     return (centre * lax.rsqrt(spread + 1e-5) * gain).astype(BF)
 
 
-def tree_place(b):
+def tree_place(b, z):
     y, q = b % 8, b // 8
     x, h = q // 2, q % 2
-    y_depth = jnp.where(y == 0, 0, jnp.where((y == 3) | (y == 6), 1, 2))
-    x_depth = jnp.where(x == 0, 0, jnp.where(x == 2, 2, 1))
+    turn = (x + 4 - h * z) % 4
+    edge = turn == 0
+    depth = jnp.where(h == 1, jnp.where(z > 0, 2, 1), 0) + jnp.where(
+        y == 0, 0, jnp.where((y == 3) | (y == 6), 1, 2))
     y_parent = jnp.where((y == 2) | (y == 5), b + 1, jnp.where((y == 1) | (y == 4), b - 1, b - y))
-    parent = jnp.where(x > 0, jnp.where(x == 3, b - 48, b - 16), jnp.where(y > 0, y_parent, b - 8))
+    parent = jnp.where(edge, jnp.where(y > 0, y_parent, b - 8), (h * z * 2 + h) * 8 + y)
     y_index = jnp.where((y == 1) | (y == 7), jnp.where(y == 1, 3, 4), jnp.where((y == 6) | (y == 4), 2, 1))
-    index = jnp.where(x > 0, jnp.where(x == 3, 6, 5), jnp.where(y > 0, y_index, 0))
-    edge = x == 0
+    index = jnp.where(edge, jnp.where(y > 0, y_index, 0), 4 + turn)
+    cross = (h == 0) & (y == 0) & (x == z)
+
+    def over_x(k):
+        return (((x + k) % 4) * 2 + h) * 8 + y
+
     children = [
-        (edge & (h == 0) & (y == 0), b + 8),
+        (cross, b + 8),
         (edge & ((y == 0) | (y == 3) | (y == 6)), jnp.where(y == 0, b + 3, b - 1)),
         (edge & ((y == 0) | (y == 3)), jnp.where(y == 0, b + 6, b + 1)),
         (edge & (y == 0), b + 1),
         (edge & (y == 0), b + 7),
-        (x <= 1, b + 16),
-        (edge, b + 48),
+        (edge, over_x(1)),
+        (edge, over_x(2)),
+        (edge, over_x(3)),
     ]
-    return h + y_depth + x_depth, parent, index, children
-
-
-TREE_ORDER = (1, 2, 3, 4, 5, 6, 0)
+    return edge, cross, depth, parent, index, children
+
+
+OWN, LANE, FAR, CROSS = range(4)
 
 
 class Net:
@@ -81,9 +88,12 @@
         self.r = lax.axis_index("row")
         self.z, self.c = self.r // 2, self.r % 2
         self.other = self.r + 1 - 2 * self.c
-        self.depth, self.parent, self.index, children = tree_place(self.b)
+        self.end = (self.z == 0) | (self.z == self.chips - 1)
+        self.edge, self.cross, self.depth, self.parent, self.index, children = tree_place(self.b, self.z)
         self.children = [(cond & (to < self.size), to) for cond, to in children]
         self.lead = g_ref.shape[0] - 1
+        self.late = self.b % 16 == 15
+        self.after_late = (self.b % 16 == 0) & (self.b > 0)
 
     def peer(self, d):
         return (self.r + d) % self.rows
@@ -98,95 +108,111 @@
 
         for d in range(1, self.rows):
             pl.semaphore_signal(barrier, inc=1, device_id=(self.b, self.peer(d)), device_id_type=MESH)
-        signal(self.b < self.size - 1, self.b + 1, self.r)
+        signal((self.b < self.size - 1) & jnp.logical_not(self.late), self.b + 1, self.r)
+        signal(self.after_late, self.b - 1, self.r)
         for cond, to in self.children:
             signal(cond, to, self.r)
 
     def greet(self):
         barrier = pltpu.get_barrier_semaphore()
-        pl.semaphore_wait(barrier, self.rows - 1 + jnp.where(self.b > 0, 2, 0))
+        early = (self.b > 0) & jnp.logical_not(self.after_late)
+        others = jnp.where(self.b > 0, 1, 0) + jnp.where(early, 1, 0)
+        others += jnp.where(self.late & (self.b < self.size - 1), 1, 0)
+        pl.semaphore_wait(barrier, self.rows - 1 + others)
+
+        @pl.when(early)
+        def _():
+            pl.semaphore_signal(self.prev_ready, inc=1, device_id=(self.b - 1, self.r), device_id_type=MESH)
 
         @pl.when(self.b > 0)
         def _():
-            pl.semaphore_signal(self.prev_ready, inc=1, device_id=(self.b - 1, self.r), device_id_type=MESH)
             pl.semaphore_signal(self.tree_ready.at[self.index], inc=1, device_id=(self.parent, self.r),
                                 device_id_type=MESH)
 
-    def row_copy(self, s, chip, kind, index):
-        to = [self.r + 2, self.r - 2, self.other][kind]
-        shard = 2 * chip + self.c
+    def shard_copy(self, s, chip, to, kind):
+        ref = self.g.at[s, self.c, chip]
         return pltpu.make_async_remote_copy(
-            src_ref=self.g.at[s, shard], dst_ref=self.g.at[s, shard],
-            send_sem=self.row_send.at[s, kind, index], recv_sem=self.recv.at[s, shard],
+            src_ref=ref, dst_ref=ref, send_sem=self.row_send.at[s], recv_sem=self.recv.at[s, kind],
             device_id=(self.b, to), device_id_type=MESH)
 
-    def arrived(self, s, shard):
-        pltpu.make_async_remote_copy(
-            src_ref=self.g.at[s, shard], dst_ref=self.g.at[s, shard],
-            send_sem=self.row_send.at[s, 0, 0], recv_sem=self.recv.at[s, shard],
-            device_id=(self.b, self.other), device_id_type=MESH).wait_recv()
-
-    def pass_on(self, s, t, right, left):
+    def several(self, s, core, count, kind):
+        ref = self.g.at[s, core, pl.ds(0, count)]
+        return pltpu.make_async_remote_copy(
+            src_ref=ref, dst_ref=ref, send_sem=self.row_send.at[s], recv_sem=self.recv.at[s, kind],
+            device_id=(self.b, self.other), device_id_type=MESH)
+
+    def spread_own(self, s):
         z, last = self.z, self.chips - 1
-        if right:
-            @pl.when(z < last)
+        two = jnp.where(self.end, FAR, LANE)
+        for step in (1, 2):
+            kind = LANE if step == 1 else two
+
+            @pl.when(z + step <= last)
             def _():
-                self.row_copy(s, z - t, 0, t).start()
-        if left:
-            @pl.when(z > 0)
+                self.shard_copy(s, z, self.r + 2 * step, kind).start()
+
+            @pl.when(z - step >= 0)
             def _():
-                self.row_copy(s, z + t, 1, t).start()
-        chip = z - t if right else z + t
-        self.row_copy(s, chip, 2, chip).start()
-
-    def step(self, s, t):
-        z, last = self.z, self.chips - 1
-        if t == 0:
-            self.pass_on(s, 0, True, True)
-            return
-
-        @pl.when(z - t >= 0)
-        def _():
-            self.arrived(s, 2 * (z - t) + self.c)
-            self.pass_on(s, t, True, False)
-
-        @pl.when(z + t <= last)
-        def _():
-            self.arrived(s, 2 * (z + t) + self.c)
-            self.pass_on(s, t, False, True)
+                self.shard_copy(s, z, self.r - 2 * step, kind).start()
+
+    def forward(self, s):
+        last = self.chips - 1
+
+        @pl.when(self.z == 1)
+        def _():
+            self.several(s, self.c, 1, FAR).wait_recv()
+            self.shard_copy(s, last, self.r - 2, LANE).start()
+
+        @pl.when(self.z == last - 1)
+        def _():
+            self.several(s, self.c, 1, FAR).wait_recv()
+            self.shard_copy(s, 0, self.r + 2, LANE).start()
+
+    def hand_over(self, s):
+        @pl.when(self.end)
+        def _():
+            self.several(s, self.c, 3, LANE).wait_recv()
+
+        @pl.when(jnp.logical_not(self.end))
+        def _():
+            self.several(s, self.c, 2, LANE).wait_recv()
+        self.several(s, self.c, self.chips, CROSS).start()
 
     def finish(self, s):
-        for chip in range(self.chips):
-            self.arrived(s, 2 * chip + 1 - self.c)
+        self.several(s, 1 - self.c, self.chips, CROSS).wait_recv()
 
     def drain(self, s):
-        z, last = self.z, self.chips - 1
-        for t in range(self.chips):
-            @pl.when((z - t >= 0) & (z < last))
-            def _():
-                self.row_copy(s, z - t, 0, t).wait_send()
-
-            @pl.when((z + t <= last) & (z > 0))
-            def _():
-                self.row_copy(s, z + t, 1, t).wait_send()
-            self.row_copy(s, t, 2, t).wait_send()
+        @pl.when(self.end)
+        def _():
+            self.several(s, self.c, 2, LANE).wait_send()
+
+        @pl.when(jnp.logical_not(self.end))
+        def _():
+            self.several(s, self.c, 4, LANE).wait_send()
+        self.several(s, self.c, self.chips, LANE).wait_send()
+
+    def own_arrived(self, s):
+        self.several(s, self.c, 1, OWN).wait_recv()
 
     def prev_copy(self):
         return pltpu.make_async_remote_copy(
-            src_ref=self.last, dst_ref=self.g.at[0, self.r],
-            send_sem=self.prev_send, recv_sem=self.recv.at[0, self.r],
+            src_ref=self.last, dst_ref=self.g.at[0, self.c, self.z],
+            send_sem=self.prev_send, recv_sem=self.recv.at[0, OWN],
             device_id=(self.b + 1, self.r), device_id_type=MESH)
 
     def prev_start(self):
+        @pl.when((self.b < self.size - 1) & jnp.logical_not(self.late))
+        def _():
+            pl.semaphore_wait(self.prev_ready, 1)
+
         @pl.when(self.b < self.size - 1)
         def _():
-            pl.semaphore_wait(self.prev_ready, 1)
             self.prev_copy().start()
 
     def prev_arrived(self):
         @pl.when(self.b > 0)
         def _():
-            self.arrived(0, self.r)
+            self.own_arrived(0)
 
     def prev_drain(self):
         @pl.when(self.b < self.size - 1)
@@ -194,31 +220,37 @@
             self.prev_copy().wait_send()
 
     def tree_copy(self, index, to):
+        ref = self.g.at[self.lead, self.c, self.z]
         return pltpu.make_async_remote_copy(
-            src_ref=self.g.at[self.lead, self.r], dst_ref=self.g.at[self.lead, self.r],
-            send_sem=self.tree_send.at[index], recv_sem=self.recv.at[self.lead, self.r],
-            device_id=(to, self.r), device_id_type=MESH)
+            src_ref=ref, dst_ref=ref, send_sem=self.tree_send.at[index],
+            recv_sem=self.recv.at[self.lead, OWN], device_id=(to, self.r), device_id_type=MESH)
+
+    def tree_one(self, index):
+        cond, to = self.children[index]
+
+        @pl.when(cond)
+        def _():
+            pl.semaphore_wait(self.tree_ready.at[index], 1)
+            self.tree_copy(index, to).start()
 
     def tree_step(self, level):
-        @pl.when(self.depth == level)
+        @pl.when(self.edge & (self.depth == level))
         def _():
             if level > 0:
-                self.arrived(self.lead, self.r)
-            for index in TREE_ORDER[:-1]:
-                cond, to = self.children[index]
-
-                @pl.when(cond)
-                def _():
-                    pl.semaphore_wait(self.tree_ready.at[index], 1)
-                    self.tree_copy(index, to).start()
-
-    def root_step(self):
-        cond, to = self.children[0]
-
-        @pl.when(cond)
-        def _():
-            pl.semaphore_wait(self.tree_ready.at[0], 1)
-            self.tree_copy(0, to).start()
+                self.own_arrived(self.lead)
+            for index in TREE_ORDER:
+                self.tree_one(index)
+
+    def cross_step(self):
+        @pl.when(self.cross & (self.b > 0))
+        def _():
+            self.own_arrived(self.lead)
+        self.tree_one(0)
+
+    def lead_arrived(self):
+        @pl.when(jnp.logical_not(self.edge | self.cross))
+        def _():
+            self.own_arrived(self.lead)
 
     def tree_drain(self):
         for index, (cond, to) in enumerate(self.children):
@@ -226,56 +258,63 @@
             def _():
                 self.tree_copy(index, to).wait_send()
 
-    def sum_copy(self, f, d):
+    def sum_copy(self, group, d):
+        a, n = group
         return pltpu.make_async_remote_copy(
-            src_ref=self.all.at[0, f], dst_ref=self.all.at[d, f],
-            send_sem=self.sum_send.at[f, d], recv_sem=self.sum_recv.at[f, d],
+            src_ref=self.all.at[0, pl.ds(a, n)], dst_ref=self.all.at[d, pl.ds(a, n)],
+            send_sem=self.sum_send.at[a], recv_sem=self.sum_recv.at[a],
             device_id=(self.b, self.peer(d)), device_id_type=MESH)
 
-    def halo_copy(self, f, side):
+    def sum_all(self, group):
+        a, n = group
+        ref = self.all.at[pl.ds(1, self.rows - 1), pl.ds(a, n)]
+        return pltpu.make_async_remote_copy(
+            src_ref=ref, dst_ref=ref, send_sem=self.sum_send.at[a], recv_sem=self.sum_recv.at[a],
+            device_id=(self.b, self.other), device_id_type=MESH)
+
+    def halo_copy(self, group, side):
+        a, n = group
         width, own = self.halo.shape[2], self.u.shape[1]
         to = self.r + 1 if side == 0 else self.r - 1
         start = own - width if side == 0 else 0
         return pltpu.make_async_remote_copy(
-            src_ref=self.u.at[f, pl.ds(start, width), :], dst_ref=self.halo.at[side, f],
-            send_sem=self.halo_send.at[f, side], recv_sem=self.halo_recv.at[f, side],
+            src_ref=self.u.at[pl.ds(a, n), pl.ds(start, width), :], dst_ref=self.halo.at[side, pl.ds(a, n)],
+            send_sem=self.halo_send.at[a, side], recv_sem=self.halo_recv.at[a, side],
             device_id=(self.b, to), device_id_type=MESH)
 
-    def edge_start(self, f):
+    def edge_start(self, group):
         for d in range(1, self.rows):
-            self.sum_copy(f, d).start()
+            self.sum_copy(group, d).start()
 
         @pl.when(self.r < self.rows - 1)
         def _():
-            self.halo_copy(f, 0).start()
+            self.halo_copy(group, 0).start()
 
         @pl.when(self.r > 0)
         def _():
-            self.halo_copy(f, 1).start()
-
-    def edge_wait(self, f):
-        for d in range(1, self.rows):
-            self.sum_copy(f, d).wait_recv()
+            self.halo_copy(group, 1).start()
+
+    def edge_wait(self, group):
+        self.sum_all(group).wait_recv()
 
         @pl.when(self.r > 0)
         def _():
-            self.halo_copy(f, 0).wait_recv()
+            self.halo_copy(group, 0).wait_recv()
 
         @pl.when(self.r < self.rows - 1)
         def _():
-            self.halo_copy(f, 1).wait_recv()
-
-    def edge_drain(self, f):
-        for d in range(1, self.rows):
-            self.sum_copy(f, d).wait_send()
+            self.halo_copy(group, 1).wait_recv()
+
+    def edge_drain(self, group):
+        self.sum_all(group).wait_send()
 
         @pl.when(self.r < self.rows - 1)
         def _():
-            self.halo_copy(f, 0).wait_send()
+            self.halo_copy(group, 0).wait_send()
 
         @pl.when(self.r > 0)
         def _():
-            self.halo_copy(f, 1).wait_send()
+            self.halo_copy(group, 1).wait_send()
 
 
 def block_kernel(head_dim, width, x_hbm, ln_hbm, wq_hbm, wk_hbm, wv_hbm, wo_hbm, gn_hbm, conv_hbm, bias_hbm,
@@ -312,14 +351,14 @@
         n_s[f] = normed
         packed = (dot(normed[:half], low) + dot(normed[half:], high)).astype(BF)
         if f + 1 < frames:
-            g_s[1 + f, net.r] = packed
+            g_s[1 + f, net.c, net.z] = packed
         else:
             last_s[...] = packed
         if f == 0:
             @pl.when(net.b == 0)
             def _():
-                g_s[0, net.r] = packed
-                g_s[lead, net.r] = packed
+                g_s[0, net.c, net.z] = packed
+                g_s[lead, net.c, net.z] = packed
 
     @pl.when(net.r == 0)
     def _():
@@ -331,13 +370,12 @@
 
     norm(0)
     net.greet()
-    net.step(1, 0)
+    net.spread_own(1)
     net.tree_step(0)
     norm(1)
+    net.spread_own(2)
     norm(frames - 1)
     norm(2)
-    net.step(1, 1)
-    net.step(2, 0)
     net.prev_start()
 
     for i in range(2, 6):
@@ -351,11 +389,10 @@
         wkv_s[0, :channels, i * wide:(i + 1) * wide] = part
         wkv_s[1, channels - cut:2 * channels - cut, i * wide:(i + 1) * wide] = part
     wo_s[...] = dot_tn(spread, w_s[3]).astype(BF)
-    net.step(1, 2)
-    net.root_step()
+    net.forward(1)
+    net.spread_own(3)
     net.tree_step(1)
-    net.step(2, 1)
-    net.step(1, 3)
+    net.cross_step()
     for f in range(frames):
         q = dot(n_s[f], wq)
         for t in range(tiles):
@@ -365,12 +402,11 @@
                 q_s[f, t, j * own:(j + 1) * own, :] = kept.astype(BF)
 
     def project(slot):
-        shards = 4
-        rows = shards * half
-        count = g_s.shape[1] // shards
+        rows = g_s.shape[2] * half
+        count = g_s.shape[1]
         inside = lax.broadcasted_iota(jnp.int32, (rows, wide), 1) % LANES
         for i in range(count):
-            packed = g_s[slot, i * shards:(i + 1) * shards].reshape(rows, 2 * channels)
+            packed = g_s[slot, i].reshape(rows, 2 * channels)
             for side in range(2):
                 view = packed[:, side * cut:side * cut + wide]
                 both = dot(view, wkv_s[side])
@@ -407,42 +443,38 @@
         wider = updated.astype(F32)
         all_s[0, f, 0:1, :] = jnp.sum(wider, axis=0, keepdims=True)
         all_s[0, f, 1:2, :] = jnp.sum(wider * wider, axis=0, keepdims=True)
-        net.edge_start(f)
         return carry
 
+    net.forward(2)
+    net.hand_over(1)
     net.tree_step(2)
     net.finish(1)
     project(1)
-    net.step(2, 2)
-    net.step(3, 0)
+    net.forward(3)
+    first(1, 0)
     net.tree_step(3)
-    first(1, 0)
-    net.step(3, 1)
+    net.hand_over(2)
     first(1, 1)
     net.tree_step(4)
-    net.step(2, 3)
+    net.lead_arrived()
+    net.spread_own(lead)
     first(1, 2)
-    net.tree_step(5)
-    net.step(lead, 0)
     net.finish(2)
     project(2)
-    net.step(3, 2)
+    net.prev_arrived()
+    net.spread_own(0)
     first(2, 0)
-    net.step(lead, 1)
+    net.hand_over(3)
     first(2, 1)
-    net.step(3, 3)
-    net.prev_arrived()
-    net.step(0, 0)
+    net.forward(lead)
     first(2, 2)
     net.finish(3)
     project(3)
-    net.step(lead, 2)
     first(3, 0)
-    net.step(0, 1)
+    net.forward(0)
     first(3, 1)
-    net.step(lead, 3)
+    net.hand_over(lead)
     first(3, 2)
-    net.step(0, 2)
     net.finish(lead)
     project(lead)
     first(0, 0)
@@ -450,15 +482,18 @@
     first(0, 2)
 
     def rest(f, carry):
-        @pl.when(f == 1)
-        def _():
-            net.step(0, 3)
+        @pl.when(f == frames - 1)
+        def _():
+            net.hand_over(0)
         return second(f, carry)
 
     lax.fori_loop(1, frames, rest, 0)
+    most, final = (1, frames - 1), (0, 1)
+    net.edge_start(most)
     net.finish(0)
     project(0)
     second(0, 0)
+    net.edge_start(final)
 
     for i in range(6, len(copies)):
         copies[i].wait()
@@ -474,9 +509,10 @@
     real = ((place >= width) | (net.r > 0)) & ((place < width + own) | (net.r < net.rows - 1))
     counted = own * net.rows * group
 
-    def convolve(start, count):
+    def convolve(group):
+        start, count = group
+        net.edge_wait(group)
         for f in range(start, start + count):
-            net.edge_wait(f)
             total = all_s[0, f]
             for d in range(1, net.rows):
                 total = total + all_s[d, f]
@@ -498,15 +534,15 @@
                 summed = summed + dot(window, conv_s[a, b])
         out_ref[start:start + count] = summed.astype(BF).reshape(count, own, channels)
 
-    convolve(1, frames - 1)
-    convolve(0, 1)
+    convolve(most)
+    convolve(final)
 
     for s in range(lead + 1):
         net.drain(s)
     net.prev_drain()
     net.tree_drain()
-    for f in range(frames):
-        net.edge_drain(f)
+    net.edge_drain(most)
+    net.edge_drain(final)
 
 
 def body(latents, ln_gain, q_weight, k_weight, v_weight, o_weight, gn_gain, conv_weight, conv_bias):
@@ -533,7 +569,7 @@
             pltpu.VMEM((4, channels, channels), BF),
             pltpu.VMEM((3, 3, channels, channels), BF),
             pltpu.VMEM((frames, own, channels), BF),
-            pltpu.VMEM((slots, rows, own // 2, 2 * channels), BF),
+            pltpu.VMEM((slots, 2, rows // 2, own // 2, 2 * channels), BF),
             pltpu.VMEM((own // 2, 2 * channels), BF),
             pltpu.VMEM((2, wide, 2 * wide), BF),
             pltpu.VMEM((wide, channels), BF),
@@ -548,14 +584,14 @@
             pltpu.VMEM((2, frames, col_count, channels), BF),
             pltpu.VMEM((3, frames, own + 2 * col_count, channels), BF),
             dma((9,)),
-            dma((slots, rows)),
-            dma((slots, 3, rows // 2)),
+            dma((slots, 4)),
+            dma((slots,)),
             dma((TREE_CHILDREN,)),
             dma,
             pltpu.SemaphoreType.REGULAR((TREE_CHILDREN,)),
             pltpu.SemaphoreType.REGULAR,
-            dma((frames, rows)),
-            dma((frames, rows)),
+            dma((frames,)),
+            dma((frames,)),
             dma((frames, 2)),
             dma((frames, 2)),
         ],

time: 71.5 us -> 63.7 us (0.89)
  the two profiles are of different devices: /device:TPU:1 before, /device:TPU:337 now
where the time goes in v4:
time: 63.7 us; the launch traced here: 63.6 us
  Pallas kernels  61.8 us (97%)
  local copies, waits for them, and re-layouts  1.78 us (3%)
    pallas_call x1, Pallas kernels, body(): pl.pallas_call(functools.partial(block_kernel, head_dim, col_count), out_...  61.8 us
    unnamed x1, local copies, waits for them, and re-layouts  1.78 us

profile of v4, /device:TPU:337, one launch (start us, length us, event | category | flops | bytes accessed | tf_op | source)
XLA Modules:
  0.0 63.6 jit_solution(11143865252443813560)
XLA Ops:
  0.0 61.8 %shard_map.91 = bf16[4,128,320]{2,1,0:T(8,128)(2,1)} custom-call(bf16[4,128,320]{2,1,0:T(8,128)(2,1)} %bitcast.3, bf16[320]{0:T(512)(128)(2,1)} %ln_hbm.1, bf16[320,320]{1,0:T(8,128)(2,1)} %wq_hbm.1, bf16[320,320]{1,0:T(8,128)(2,1)} %wk_hbm.1, bf16[320,320]{1,0:T(8,128)(2,1)} %wv_hbm.1, bf16[320,320]{1,0:T(8,128)(2,1)} %wo_hbm.1, bf16[320]{0:T(512)(128)(2,1)} %gn_hbm.1, ...), custom_call_target="tpu_custom_call" | custom-call | tf_op jit(solution)/shard_map/pallas_call | solution.py:559
  61.8 1.8 %copy.11 = bf16[4,4,32,320]{3,2,1,0:T(8,128)(2,1)} copy(bf16[4,4,32,320]{3,2,1,0:T(8,128)(2,1)} %bitcast.2) | data formatting | bytes 655360

commit v5 on v4

--- a/solution.py
+++ b/solution.py
@@ -449,13 +449,13 @@
     net.hand_over(1)
     net.tree_step(2)
     net.finish(1)
+    net.tree_step(3)
     project(1)
     net.forward(3)
     first(1, 0)
-    net.tree_step(3)
+    net.tree_step(4)
     net.hand_over(2)
     first(1, 1)
-    net.tree_step(4)
     net.lead_arrived()
     net.spread_own(lead)
     first(1, 2)

time: 63.7 us -> 63.7 us (level)
  no operation moved by 1% of the time
where the time goes in v5:
time: 63.7 us; the launch traced here: 63.6 us
  Pallas kernels  61.8 us (97%)
  local copies, waits for them, and re-layouts  1.78 us (3%)
    pallas_call x1, Pallas kernels, body(): pl.pallas_call(functools.partial(block_kernel, head_dim, col_count), out_...  61.8 us
    unnamed x1, local copies, waits for them, and re-layouts  1.78 us

profile of v5, /device:TPU:337, one launch (start us, length us, event | category | flops | bytes accessed | tf_op | source)
XLA Modules:
  0.0 63.6 jit_solution(4979205109005432391)
XLA Ops:
  0.0 61.8 %shard_map.91 = bf16[4,128,320]{2,1,0:T(8,128)(2,1)} custom-call(bf16[4,128,320]{2,1,0:T(8,128)(2,1)} %bitcast.3, bf16[320]{0:T(512)(128)(2,1)} %ln_hbm.1, bf16[320,320]{1,0:T(8,128)(2,1)} %wq_hbm.1, bf16[320,320]{1,0:T(8,128)(2,1)} %wk_hbm.1, bf16[320,320]{1,0:T(8,128)(2,1)} %wv_hbm.1, bf16[320,320]{1,0:T(8,128)(2,1)} %wo_hbm.1, bf16[320]{0:T(512)(128)(2,1)} %gn_hbm.1, ...), custom_call_target="tpu_custom_call" | custom-call | tf_op jit(solution)/shard_map/pallas_call | solution.py:559
  61.8 1.8 %copy.11 = bf16[4,4,32,320]{3,2,1,0:T(8,128)(2,1)} copy(bf16[4,4,32,320]{3,2,1,0:T(8,128)(2,1)} %bitcast.2) | data formatting | bytes 655360
